TPU v7x, 32 devices: a whole 2x2x4 slice. The times are simulated.
32 devices in a mesh: grp: 2 (over x), tm: 8 (over z, y), blk: 2 (over core).
Axes of the slice: x: 2, y: 2, z: 4, core: 2. Of those that a mesh axis runs over, the one named last changes fastest.
Arguments:
- hyper_params: float32 [6], P('grp'), parts along dimension 0, as said below
- space_precision: float32 [256, 256], P('blk'), may hold values from -1 to 16, as said below
- data_precision: float32 [32, 256, 256], P(('grp', 'tm'), 'blk'), parts along dimension 0, may hold values from -1 to 4, as said below
- covariates: float32 [32, 32, 256], P(('grp', 'tm'), None, 'blk'), parts along dimension 0
- fixed_precision: float32 [64], P('grp'), parts along dimension 0, may hold values from 0.5 to 2
Outputs:
- day_covariance: float32 [32, 256, 256], P(('grp', 'tm'), 'blk'), parts along dimension 0
- day_gradients: float32 [3, 32], P(None, ('grp', 'tm')), parts along dimension 1
- fixed_covariance: float32 [64, 32], P('grp'), parts along dimension 0
There are 2 independent parts, one for each index of `grp`. A program takes and returns all parts, laid end to end along the dimension named above; an argument that names none is the same for every part. Nothing has to cross between parts.
Inputs may be any that keep to these rules, and one draw needn't show every extreme that they name: `hyper_params`: entries 0 and 2 lie in -0.3 to 0.3; entry 1 equals atanh(1 - e) with e between 1.5 / 16 and 6 / 16. `space_precision`: symmetric positive definite. `data_precision`: each day's block is symmetric positive definite.
All inputs are finite; a program needn't handle non-finite values.
Results may differ from a plain program's by a relative error of at most 0.0003.
Values sent between devices are 32-bit elements; how exact they have to be, the bound alone decides.
A program may use at most 128 MiB of HBM per device.

v0:
```python
import jax
import jax.numpy as jnp
from jax import lax
from jax.sharding import PartitionSpec as P

HIGHEST = lax.Precision.HIGHEST


def passed_along(block, axis, distance):
    devices = range(lax.axis_size(axis))
    route = [(i - distance, i) for i in devices if i - distance in devices]
    return lax.ppermute(block, axis, route)


def product(multiplier, multiplicand):
    return jnp.dot(multiplier, multiplicand, precision=HIGHEST, preferred_element_type=jnp.float32)


def frobenius(matrix_one, matrix_two):
    return jnp.sum(matrix_one * matrix_two)


def columns_of(matrix, column_start, breadth):
    return lax.dynamic_slice_in_dim(matrix, column_start, breadth, 1)


def rows_of(matrix, column_start, breadth):
    return lax.dynamic_slice_in_dim(matrix, column_start, breadth, 0)


def assemble(packet, heights):
    gathered = lax.all_gather(packet, "blk", axis=1, tiled=True)
    pieces = []
    offset = 0
    for height in heights:
        pieces.append(gathered[offset : offset + height])
        offset += height
    return pieces


def neighbour(packet, distance):
    return passed_along(packet, "tm", distance)


def fixed_total(local_sum):
    return lax.psum(local_sum, "tm")


def inverse_full(matrix):
    factor = jnp.linalg.cholesky(matrix)
    identity = jnp.eye(matrix.shape[0], dtype=jnp.float32)
    return jax.scipy.linalg.cho_solve((factor, True), identity)


def guarded(predicate, compute, template):
    return lax.cond(predicate, compute, lambda: jax.tree.map(jnp.zeros_like, template))


def eliminate_all(inverse, left_link, right_link, side_link, column_start, breadth):
    inverse_left = product(inverse, columns_of(left_link, column_start, breadth))
    toward_left = -product(left_link.T, inverse_left)
    inverse_right = product(inverse, rows_of(right_link, column_start, breadth).T)
    toward_right = -product(right_link, inverse_right)
    fill_link = -product(right_link, inverse_left)
    side_inverse = product(side_link, inverse)
    left_side = -product(side_inverse, left_link)
    right_side = -product(side_inverse, right_link.T)
    own_term = product(side_inverse, side_link.T)
    return (toward_left, toward_right, fill_link, left_side, right_side, own_term)


def back_terms(
    inverse,
    left_link,
    right_link,
    side_link,
    left_self,
    left_side,
    right_self,
    right_side,
    between,
    fixed_sigma,
    column_start,
    breadth,
):
    combined_left = (
        product(left_link, columns_of(left_self, column_start, breadth))
        + product(right_link.T, rows_of(between, column_start, breadth).T)
        + product(side_link.T, columns_of(left_side, column_start, breadth))
    )
    cross_left = -product(inverse, combined_left)
    combined_right = (
        product(left_link, columns_of(between, column_start, breadth))
        + product(right_link.T, columns_of(right_self, column_start, breadth))
        + product(side_link.T, columns_of(right_side, column_start, breadth))
    )
    cross_right = -product(inverse, combined_right)
    side_new = -product(
        product(left_side, left_link.T)
        + product(right_side, right_link)
        + product(fixed_sigma, side_link),
        inverse,
    )
    inverse_part = columns_of(inverse, column_start, breadth)
    left_times = product(left_link.T, inverse_part)
    right_times = product(right_link, inverse_part)
    side_times = product(side_link, inverse_part)
    column_left = -(
        product(left_self, left_times)
        + product(between, right_times)
        + product(left_side.T, side_times)
    )
    column_right = -(
        product(between.T, left_times)
        + product(right_self, right_times)
        + product(right_side.T, side_times)
    )
    self_half = inverse_part - product(
        inverse,
        product(left_link, column_left)
        + product(right_link.T, column_right)
        + product(side_link.T, columns_of(side_new, column_start, breadth)),
    )
    return (cross_left, cross_right, side_new, self_half)


def on_device(hyper_params, space_precision, data_precision, covariates, fixed_precision):
    spatial, observed, design = (
        lax.all_gather(space_precision, "blk", axis=0, tiled=True),
        lax.all_gather(data_precision, "blk", axis=1, tiled=True),
        lax.all_gather(covariates, "blk", axis=2, tiled=True),
    )
    extent = spatial.shape[0]
    days_here = observed.shape[0]
    fixed_count = design.shape[1]
    breadth = extent // lax.axis_size("blk")
    column_start = lax.axis_index("blk") * breadth
    device_count = lax.axis_size("tm")
    position = lax.axis_index("tm")
    level_count = device_count.bit_length() - 1
    ordinal = position + 1
    prior_scale = jnp.exp(hyper_params[0])
    correlation = jnp.tanh(hyper_params[1])
    noise_scale = jnp.exp(hyper_params[2])
    complement = 1.0 - correlation * correlation
    couple = -prior_scale * correlation * spatial
    day_index = position * days_here + jnp.arange(days_here)
    border = (day_index == 0) | (day_index == days_here * device_count - 1)
    weight = jnp.where(border, 1.0, 1.0 + correlation * correlation)
    weight_rate = jnp.where(border, 0.0, 2.0 * correlation * complement)
    blocks = prior_scale * weight[:, None, None] * spatial[None] + noise_scale * observed
    arrow_blocks = noise_scale * jnp.einsum(
        "dfi,dij->dfj", design, observed, precision=HIGHEST, preferred_element_type=jnp.float32
    )
    data_gram = jnp.einsum(
        "dfj,dgj->fg", arrow_blocks, design, precision=HIGHEST, preferred_element_type=jnp.float32
    )
    empty_half = jnp.zeros((extent, breadth), jnp.float32)
    empty_side = jnp.zeros((fixed_count, extent), jnp.float32)
    empty_small = jnp.zeros((fixed_count, fixed_count), jnp.float32)
    empty_full = jnp.zeros((extent, extent), jnp.float32)
    start_link = jnp.where(position > 0, couple, empty_full)

    def forward_step(index_day, carried):
        blocks_now, arrows_now, current, left_sum, side_sum, arrow_terms, inverses, left_links = (
            carried
        )
        square = lax.dynamic_index_in_dim(blocks_now, index_day, 0, keepdims=False)
        side_link = lax.dynamic_index_in_dim(arrows_now, index_day, 0, keepdims=False)
        inverse = inverse_full(square)
        toward_left, toward_right, fill_link, left_side, right_side, own_term = eliminate_all(
            inverse, current, couple, side_link, column_start, breadth
        )
        toward_left, toward_right, fill_link = assemble(
            jnp.concatenate([toward_left, toward_right, fill_link], 0), [extent, extent, extent]
        )
        blocks_now = blocks_now.at[index_day + 1].add(toward_right)
        arrows_now = arrows_now.at[index_day + 1].add(right_side)
        inverses = inverses.at[index_day].set(inverse)
        left_links = left_links.at[index_day].set(current)
        return (
            blocks_now,
            arrows_now,
            fill_link,
            left_sum + toward_left,
            side_sum + left_side,
            arrow_terms - own_term,
            inverses,
            left_links,
        )

    initial = (
        blocks,
        arrow_blocks,
        start_link,
        empty_full,
        empty_side,
        empty_small,
        jnp.zeros_like(blocks),
        jnp.zeros_like(blocks),
    )
    (
        blocks_final,
        arrows_final,
        border_link,
        left_sum,
        side_sum,
        arrow_terms,
        inverses,
        left_links,
    ) = lax.fori_loop(0, days_here - 1, forward_step, initial)
    gram_total = fixed_total(data_gram)
    arrived = neighbour(
        jnp.concatenate(
            [
                columns_of(left_sum, column_start, breadth),
                columns_of(side_sum, column_start, breadth),
            ],
            0,
        ),
        -1,
    )
    incoming_block, incoming_side = assemble(arrived, [extent, fixed_count])
    border_block = blocks_final[days_here - 1] + incoming_block
    border_side = arrows_final[days_here - 1] + incoming_side
    saved_inverse = empty_full
    saved_left = empty_full
    saved_side = empty_side
    saved_right = empty_full
    for level_index in range(level_count):
        distance = 1 << level_index
        leaving = (ordinal % distance == 0) & (ordinal // distance % 2 == 1)
        staying = ordinal % (2 * distance) == 0
        inverse = guarded(leaving, lambda: inverse_full(border_block), empty_full)
        arrived = neighbour(columns_of(border_link, column_start, breadth), -distance)
        (right_link,) = assemble(arrived, [extent])
        toward_left, toward_right, fill_link, left_side, right_side, own_term = guarded(
            leaving,
            lambda: eliminate_all(
                inverse, border_link, right_link, border_side, column_start, breadth
            ),
            (empty_half, empty_half, empty_half, empty_side, empty_side, empty_small),
        )
        arrived_right = neighbour(
            jnp.concatenate(
                [toward_right, fill_link, columns_of(right_side, column_start, breadth)], 0
            ),
            distance,
        )
        arrived_left = neighbour(
            jnp.concatenate([toward_left, columns_of(left_side, column_start, breadth)], 0),
            -distance,
        )
        incoming_right, incoming_fill, incoming_right_side, incoming_left, incoming_left_side = (
            assemble(
                jnp.concatenate([arrived_right, arrived_left], 0),
                [extent, extent, fixed_count, extent, fixed_count],
            )
        )
        saved_right = jnp.where(leaving, right_link, saved_right)
        saved_inverse = jnp.where(leaving, inverse, saved_inverse)
        saved_left = jnp.where(leaving, border_link, saved_left)
        saved_side = jnp.where(leaving, border_side, saved_side)
        arrow_terms = arrow_terms - jnp.where(leaving, own_term, 0.0)
        border_block = border_block + jnp.where(staying, incoming_right + incoming_left, 0.0)
        border_side = border_side + jnp.where(
            staying, incoming_right_side + incoming_left_side, 0.0
        )
        border_link = jnp.where(staying, incoming_fill, border_link)
    root_device = position == device_count - 1
    root_inverse = guarded(root_device, lambda: inverse_full(border_block), empty_full)
    root_side = product(border_side, root_inverse)
    arrow_terms = arrow_terms - jnp.where(root_device, product(root_side, border_side.T), 0.0)
    schur_sum = gram_total + fixed_total(arrow_terms)
    schur_matrix = jnp.diag(fixed_precision) + schur_sum
    fixed_sigma = inverse_full(schur_matrix)
    sigma_half = jnp.where(
        root_device,
        columns_of(root_inverse, column_start, breadth)
        + product(root_side.T, product(fixed_sigma, columns_of(root_side, column_start, breadth))),
        0.0,
    )
    sigma_side = jnp.where(root_device, -product(fixed_sigma, root_side), 0.0)
    left_cross = empty_half
    right_cross = empty_half
    for level_index in reversed(range(level_count)):
        distance = 1 << level_index
        leaving = (ordinal % distance == 0) & (ordinal // distance % 2 == 1)
        arrived_left = neighbour(
            jnp.concatenate(
                [sigma_half, columns_of(sigma_side, column_start, breadth), right_cross], 0
            ),
            distance,
        )
        arrived_right = neighbour(
            jnp.concatenate(
                [sigma_half, columns_of(sigma_side, column_start, breadth), left_cross], 0
            ),
            -distance,
        )
        left_self, left_side, left_right, right_self, right_side, right_left = assemble(
            jnp.concatenate([arrived_left, arrived_right], 0),
            [extent, fixed_count, extent, extent, fixed_count, extent],
        )
        coupling = saved_right
        right_leaves = (ordinal + distance) // (2 * distance) % 2 == 1
        between = jnp.where(right_leaves, right_left.T, left_right)
        cross_left, cross_right, side_new, self_half = guarded(
            leaving,
            lambda: back_terms(
                saved_inverse,
                saved_left,
                coupling,
                saved_side,
                left_self,
                left_side,
                right_self,
                right_side,
                between,
                fixed_sigma,
                column_start,
                breadth,
            ),
            (empty_half, empty_half, empty_side, empty_half),
        )
        sigma_half = jnp.where(leaving, self_half, sigma_half)
        sigma_side = jnp.where(leaving, side_new, sigma_side)
        left_cross = jnp.where(leaving, cross_left, left_cross)
        right_cross = jnp.where(leaving, cross_right, right_cross)
    arrived = neighbour(
        jnp.concatenate(
            [sigma_half, columns_of(sigma_side, column_start, breadth), right_cross], 0
        ),
        1,
    )
    earlier_self, earlier_side, earlier_right, own_self, own_left = assemble(
        jnp.concatenate([arrived, sigma_half, left_cross], 0),
        [extent, fixed_count, extent, extent, extent],
    )
    own_cross = jnp.where(position % 2 == 0, own_left, earlier_right.T)
    own_cross = jnp.where(position > 0, own_cross, 0.0)
    rows_out = jnp.zeros((days_here, breadth, extent), jnp.float32)
    rows_out = rows_out.at[days_here - 1].set(sigma_half.T)
    stat_block = jnp.zeros((4, days_here), jnp.float32)
    stat_block = stat_block.at[0, days_here - 1].set(frobenius(own_self, spatial))
    stat_block = stat_block.at[1, days_here - 1].set(frobenius(own_self, observed[days_here - 1]))
    stat_block = stat_block.at[2, days_here - 1].set(
        frobenius(sigma_side, arrow_blocks[days_here - 1])
    )

    def backward_step(count_done, carried):
        next_self, next_side, next_cross, rows_now, stats_now = carried
        index_day = days_here - 2 - count_done
        inverse = lax.dynamic_index_in_dim(inverses, index_day, 0, keepdims=False)
        left_link = lax.dynamic_index_in_dim(left_links, index_day, 0, keepdims=False)
        side_link = lax.dynamic_index_in_dim(arrows_final, index_day, 0, keepdims=False)
        observed_day = lax.dynamic_index_in_dim(observed, index_day, 0, keepdims=False)
        arrow_day = lax.dynamic_index_in_dim(arrow_blocks, index_day, 0, keepdims=False)
        cross_left, cross_right, side_new, self_half = back_terms(
            inverse,
            left_link,
            couple,
            side_link,
            earlier_self,
            earlier_side,
            next_self,
            next_side,
            next_cross.T,
            fixed_sigma,
            column_start,
            breadth,
        )
        self_full, cross_left_full, cross_right_full = assemble(
            jnp.concatenate([self_half, cross_left, cross_right], 0), [extent, extent, extent]
        )
        stats_now = stats_now.at[0, index_day].set(frobenius(self_full, spatial))
        stats_now = stats_now.at[1, index_day].set(frobenius(self_full, observed_day))
        stats_now = stats_now.at[2, index_day].set(frobenius(side_new, arrow_day))
        stats_now = stats_now.at[3, index_day + 1].set(frobenius(cross_right_full.T, spatial))
        rows_now = rows_now.at[index_day].set(self_half.T)
        return (self_full, side_new, cross_left_full, rows_now, stats_now)

    back_start = (own_self, sigma_side, own_cross, rows_out, stat_block)
    last_self, last_side, first_cross, rows_out, stat_block = lax.fori_loop(
        0, days_here - 1, backward_step, back_start
    )
    stat_block = stat_block.at[3, 0].set(
        jnp.where(position > 0, frobenius(first_cross, spatial), 0.0)
    )
    trace_space = stat_block[0]
    trace_data = stat_block[1]
    trace_side = stat_block[2]
    trace_cross = stat_block[3]
    gradients = (
        jnp.stack(
            [
                prior_scale * weight * trace_space - 2.0 * prior_scale * correlation * trace_cross,
                prior_scale * weight_rate * trace_space
                - 2.0 * prior_scale * complement * trace_cross,
                noise_scale * trace_data + 2.0 * trace_side,
            ]
        )
        / extent
    )
    return (rows_out, gradients, fixed_sigma)


def solution(mesh):
    in_specs = (
        P("grp"),
        P("blk", None),
        P(("grp", "tm"), "blk", None),
        P(("grp", "tm"), None, "blk"),
        P("grp"),
    )
    out_specs = (P(("grp", "tm"), "blk", None), P(None, ("grp", "tm")), P("grp", None))
    return jax.shard_map(
        on_device, mesh=mesh, in_specs=in_specs, out_specs=out_specs, check_vma=False
    )
```

profile of v0, /device:TPU:0, one launch (start us, length us, event | category | flops | bytes accessed | tf_op | source)
XLA Modules:
  0.0 723.9 jit_solution(16666559431165720687)
XLA Ops:
  10.7 2.5 all_gather.51
  17.0 11.7 %cholesky.428 = f32[128,128]{1,0:T(8,128)S(1)} custom-call(f32[128,128]{1,0:T(8,128)S(1)} %cholesky.470), custom_call_target="Cholesky" | custom-call | tf_op jit(solution)/shard_map/while/body/eval_jaxpr/jit(cholesky)/cholesky | solution.py:50
  28.7 9.8 %custom-call.40 = f32[1,128,128]{1,2,0:T(8,128)S(1)} custom-call(f32[1,128,128]{2,1,0:T(8,128)S(1)} %get-tuple-element.1168), custom_call_target="InvertDiagBlocksLowerTriangular" | custom-call | tf_op jit(solution)/shard_map/while/body/eval_jaxpr/jit(cholesky)/cholesky | solution.py:50
  39.1 11.7 %cholesky.445 = f32[128,128]{1,0:T(8,128)S(1)} custom-call(f32[128,128]{1,0:T(8,128)S(1)} %convolution_subtract_fusion.15), custom_call_target="Cholesky" | custom-call | tf_op jit(solution)/shard_map/while/body/eval_jaxpr/jit(cholesky)/cholesky | solution.py:50
  53.5 4.2 while.49
  57.7 19.7 %custom-call.41 = f32[2,128,128]{1,2,0:T(8,128)S(1)} custom-call(f32[2,128,128]{2,1,0:T(8,128)S(1)} %get-tuple-element.945), custom_call_target="InvertDiagBlocksLowerTriangular" | custom-call | tf_op jit(solution)/shard_map/while/body/eval_jaxpr/jit(_cho_solve)/triangular_solve | solution.py:52
  81.4 2.4 all_gather.52
  90.1 2.4 collective-permute-done.1
  92.5 2.3 all_gather.55
  94.8 3.7 collective-permute-done
  98.5 2.3 all_gather.54
  103.1 67.5 %conditional.10 = (f32[256,256]{1,0:T(8,128)S(1)}) conditional(s32[]{:T(128)} %convert_element_type.36, () %tuple.183, f32[256,256]{0,1:T(8,128)S(1)} %fusion.242), branch_computations={%region_4.7_spmd, %region_5.8_spmd} | conditional | flops 353124608 | bytes 8325411 | solution.py:56
  103.5 11.7 %cholesky.292 = f32[128,128]{1,0:T(8,128)S(1)} custom-call(f32[128,128]{1,0:T(8,128)S(1)} %cholesky.458), custom_call_target="Cholesky" | custom-call | tf_op jit(solution)/shard_map/cond/branch_1_fun/jit(cholesky)/cholesky | solution.py:50
  115.3 9.8 %custom-call.32 = f32[1,128,128]{1,2,0:T(8,128)S(1)} custom-call(f32[1,128,128]{2,1,0:T(8,128)S(1)} %get-tuple-element.1113), custom_call_target="InvertDiagBlocksLowerTriangular" | custom-call | tf_op jit(solution)/shard_map/cond/branch_1_fun/jit(cholesky)/cholesky | solution.py:50
  127.3 11.7 %cholesky.309 = f32[128,128]{1,0:T(8,128)S(1)} custom-call(f32[128,128]{1,0:T(8,128)S(1)} %convolution_subtract_fusion.2), custom_call_target="Cholesky" | custom-call | tf_op jit(solution)/shard_map/cond/branch_1_fun/jit(cholesky)/cholesky | solution.py:50
  141.1 4.2 while.45
  146.0 20.5 %custom-call.33 = f32[2,128,128]{1,2,0:T(8,128)S(1)} custom-call(f32[2,128,128]{2,1,0:T(8,128)} %copy-done.46), custom_call_target="InvertDiagBlocksLowerTriangular" | custom-call | tf_op jit(solution)/shard_map/cond/branch_1_fun/jit(_cho_solve)/triangular_solve | solution.py:52
  170.6 9.8 %conditional.11 = (f32[32,256]{1,0:T(8,128)S(1)}, f32[32,256]{1,0:T(8,128)}, f32[32,32]{1,0:T(8,128)S(1)}, f32[256,128]{1,0:T(8,128)S(1)}, f32[256,128]{1,0:T(8,128)}, /*index=5*/f32[256,128]{1,0:T(8,128)}) conditional(s32[]{:T(128)} %convert_element_type.36, () %tuple.182, (s32[]{:T(128)}, f32[256,256]{1,0:T(8,128)S(1)}, f32[256,256]{1,0:T(8,128)S(1)}, ...), branch_computations={%region_6.9_spmd, %region_7.10_spmd} | conditional | flops 582074368 | bytes 4460634 | solution.py:56
  186.3 9.2 %collective-permute-done.3 = f32[288,128]{1,0:T(8,128)} collective-permute-done((f32[288,128]{1,0:T(8,128)S(1)}, f32[288,128]{1,0:T(8,128)}, u32[]{:S(2)}, u32[]{:S(2)}) %collective-permute-start.3) | collective-permute-done | bytes 147488 | tf_op jit(solution)/shard_map/ppermute | solution.py:12
  196.6 2.4 all_gather.56
  202.0 3.1 conditional.12
  206.5 4.8 collective-permute-done.4
  216.3 4.3 collective-permute-start.5
  222.7 6.2 collective-permute-done.6
  229.9 2.4 all_gather.58
  238.0 3.3 conditional.14
  242.7 5.5 collective-permute-done.7
  250.5 3.2 conditional.15
  263.6 7.4 %collective-permute-done.9 = f32[288,128]{1,0:T(8,128)} collective-permute-done((f32[288,128]{1,0:T(8,128)S(1)}, f32[288,128]{1,0:T(8,128)}, u32[]{:S(2)}, u32[]{:S(2)}) %collective-permute-start.9) | collective-permute-done | bytes 147488 | tf_op jit(solution)/shard_map/ppermute | solution.py:12
  272.1 2.5 all_gather.60
  276.8 7.2 conditional.16
  286.6 236.7 %psum.16 = f32[32,32]{1,0:T(8,128)S(1)} all-reduce(f32[32,32]{1,0:T(8,128)} %fusion.228), channel_id=1, replica_groups=mesh['grp'=2,'tm'=8,'blk'=2] {'tm'}, use_global_device_ids=true, to_apply=%region_18.21 | all-reduce | flops 1024 | bytes 8192 | tf_op jit(solution)/shard_map/psum | solution.py:46
  527.4 3.6 cholesky.97
  532.9 3.2 custom-call.23
  541.8 2.8 collective-permute-done.10
  544.6 7.6 %collective-permute-done.11 = f32[544,128]{1,0:T(8,128)S(1)} collective-permute-done((f32[544,128]{1,0:T(8,128)S(1)}, f32[544,128]{1,0:T(8,128)S(1)}, u32[]{:S(2)}, u32[]{:S(2)}) %collective-permute-start.11) | collective-permute-done | bytes 278560 | tf_op jit(solution)/shard_map/ppermute | solution.py:12
  553.3 6.3 all-gather.5.cloned.1.call-done
  562.3 3.7 collective-permute-start.12
  567.3 5.0 collective-permute-done.12
  572.4 4.1 collective-permute-done.13
  577.4 20.5 %all-gather.7.cloned.1.call-done = f32[1088,256]{1,0:T(8,128)} async-done(((f32[1088,128]{1,0:T(8,128)}), f32[1088,256]{1,0:T(8,128)}) %all-gather.7.cloned.1.call-update) | async-done | bytes 1114128 | tf_op jit(solution)/shard_map/all_gather | solution.py:32
  601.9 23.5 %collective-permute-start.14 = (f32[544,128]{1,0:T(8,128)S(1)}, f32[544,128]{1,0:T(8,128)S(1)}, u32[]{:S(2)}, u32[]{:S(2)}) collective-permute-start(f32[544,128]{1,0:T(8,128)S(1)} %get-tuple-element.1161), channel_id=1, source_target_pairs={{0,2},{2,4},{4,6},{6,8},{8,10},{10,12},{12,14},{1,3},{3,5},{5,7},{... | collective-permute-start | bytes 835592 | tf_op jit(solution)/shard_map/ppermute | solution.py:12
  626.7 10.9 %collective-permute-done.14 = f32[544,128]{1,0:T(8,128)S(1)} collective-permute-done((f32[544,128]{1,0:T(8,128)S(1)}, f32[544,128]{1,0:T(8,128)S(1)}, u32[]{:S(2)}, u32[]{:S(2)}) %collective-permute-start.14) | collective-permute-done | bytes 278560 | tf_op jit(solution)/shard_map/ppermute | solution.py:12
  638.4 10.2 %all-gather.9.cloned.1.call-done = f32[1088,256]{1,0:T(8,128)} async-done(((f32[1088,128]{1,0:T(8,128)}), f32[1088,256]{1,0:T(8,128)}) %all-gather.9.cloned.1.call-update) | async-done | bytes 1114128 | tf_op jit(solution)/shard_map/all_gather | solution.py:32
  649.6 17.5 %conditional.19 = (f32[32,256]{1,0:T(8,128)}, f32[256,128]{1,0:T(8,128)S(1)}, f32[256,128]{1,0:T(8,128)}, f32[256,128]{1,0:T(8,128)}) conditional(s32[]{:T(128)} %convert_element_type.36, () %tuple.176, (f32[1088,256]{1,0:T(8,128)}, s32[]{:T(128)}, f32[256,256]{1,0:T(8,128)S(1)}, s32[]{:T(128)}, f32[256,256]{0,1:T(8,128)S(1)}, ...), branch_computations={%region_26.29_spmd, %region_27.30_spmd} | conditional | flops 1664671744 | bytes 19763564 | solution.py:56
  670.6 6.2 collective-permute-done.16
  681.7 9.3 %all-gather.11.cloned.1.call-done = f32[1056,256]{1,0:T(8,128)} async-done(((f32[1056,128]{1,0:T(8,128)}), f32[1056,256]{1,0:T(8,128)}) %all-gather.11.cloned.1.call-update) | async-done | bytes 1081360 | tf_op jit(solution)/shard_map/all_gather | solution.py:32
  704.5 2.5 all_gather.65
  (373 shorter events, 166.8 us)
Async XLA Ops:
  7.2 552.4 %all-gather.5.cloned.1.call-start = ((), (), s32[]{:S(2)}) async-start(), calls=%async_computation | async-start | bytes 1671168 | tf_op jit(solution)/shard_map/all_gather | solution.py:32
  13.2 0.9 copy-start.39
  16.1 63.1 %copy-start.1 = (f32[256,256]{1,0:T(8,128)}, f32[256,256]{1,0:T(8,128)S(1)}, u32[]{:S(2)}) copy-start(f32[256,256]{1,0:T(8,128)S(1)} %all_gather.50) | copy-start | bytes 786436
  16.3 22.2 %copy-start.6 = (f32[2,256,256]{1,2,0:T(8,128)}, f32[2,256,256]{1,2,0:T(8,128)S(1)}, u32[]{:S(2)}) copy-start(f32[2,256,256]{1,2,0:T(8,128)S(1)} %multiply_add_fusion) | copy-start | bytes 1572868
  83.7 115.2 %copy-start = (f32[768,256]{1,0:T(8,128)}, f32[768,256]{1,0:T(8,128)S(1)}, u32[]{:S(2)}) copy-start(f32[768,256]{1,0:T(8,128)S(1)} %all_gather.52) | copy-start | bytes 2359300
  83.7 1.4 copy-start.45
  83.8 8.7 %collective-permute-start.1 = (f32[256,128]{1,0:T(8,128)S(1)}, f32[256,128]{1,0:T(8,128)}, u32[]{:S(2)}, u32[]{:S(2)}) collective-permute-start(f32[256,128]{1,0:T(8,128)S(1)} %constant_dynamic-slice_fusion.17), channel_id=1, source_target_pairs={{2,0},{4,2},{6,4},{8,6},{10,8},{12,10},{14,12},{3,1},{5,3},{7,5},{... | collective-permute-start | bytes 393224 | tf_op jit(solution)/shard_map/ppermute | solution.py:12
  87.0 7.8 %copy-start.20 = (f32[2,32,256]{2,1,0:T(8,128)}, f32[2,32,256]{2,1,0:T(8,128)S(1)}, u32[]{:S(2)}) copy-start(f32[2,32,256]{2,1,0:T(8,128)S(1)} %all_gather.53) | copy-start | bytes 196612
  87.7 7.1 copy-start.26
  88.6 9.9 %collective-permute-start = (f32[288,128]{1,0:T(8,128)}, f32[288,128]{1,0:T(8,128)}, u32[]{:S(2)}, u32[]{:S(2)}) collective-permute-start(f32[288,128]{1,0:T(8,128)} %pad_maximum_fusion.24), channel_id=1, source_target_pairs={{2,0},{4,2},{6,4},{8,6},{10,8},{12,10},{14,12},{3,1},{5,3},{7,5},{... | collective-permute-start | bytes 442376 | tf_op jit(solution)/shard_map/ppermute | solution.py:12
  103.5 11.8 %copy-start.18 = (f32[256,256]{1,0:T(8,128)}, f32[256,256]{1,0:T(8,128)S(1)}, u32[]{:S(2)}) copy-start(f32[256,256]{1,0:T(8,128)S(1)} %fusion.165) | copy-start | bytes 786436 | tf_op jit(solution)/shard_map/cond
  180.4 18.6 %copy-start.42 = (f32[32,32]{1,0:T(8,128)}, f32[32,32]{1,0:T(8,128)S(1)}, u32[]{:S(2)}) copy-start(f32[32,32]{1,0:T(8,128)S(1)} %get-tuple-element.846) | copy-start | bytes 12292
  182.1 13.4 %collective-permute-start.2 = (f32[544,128]{1,0:T(8,128)S(1)}, f32[544,128]{1,0:T(8,128)}, u32[]{:S(2)}, u32[]{:S(2)}) collective-permute-start(f32[544,128]{1,0:T(8,128)S(1)} %pad_maximum_fusion.14), channel_id=1, source_target_pairs={{0,2},{2,4},{4,6},{6,8},{8,10},{10,12},{12,14},{1,3},{3,5},{5,7},{... | collective-permute-start | bytes 835592 | tf_op jit(solution)/shard_map/ppermute | solution.py:12
  185.0 10.5 %collective-permute-start.3 = (f32[288,128]{1,0:T(8,128)S(1)}, f32[288,128]{1,0:T(8,128)}, u32[]{:S(2)}, u32[]{:S(2)}) collective-permute-start(f32[288,128]{1,0:T(8,128)S(1)} %pad_maximum_fusion.25), channel_id=1, source_target_pairs={{2,0},{4,2},{6,4},{8,6},{10,8},{12,10},{14,12},{3,1},{5,3},{7,5},{... | collective-permute-start | bytes 442376 | tf_op jit(solution)/shard_map/ppermute | solution.py:12
  199.0 0.9 copy-start.5
  200.8 10.6 %collective-permute-start.4 = (f32[256,128]{1,0:T(8,128)}, f32[256,128]{1,0:T(8,128)}, u32[]{:S(2)}, u32[]{:S(2)}) collective-permute-start(f32[256,128]{1,0:T(8,128)} %constant_dynamic-slice_fusion.14), channel_id=1, source_target_pairs={{4,0},{6,2},{8,4},{10,6},{12,8},{14,10},{5,1},{7,3},{9,5},{11,7},{... | collective-permute-start | bytes 393224 | tf_op jit(solution)/shard_map/ppermute | solution.py:12
  214.9 17.5 %copy-start.43 = (f32[32,32]{1,0:T(8,128)}, f32[32,32]{1,0:T(8,128)S(1)}, u32[]{:S(2)}) copy-start(f32[32,32]{1,0:T(8,128)S(1)} %get-tuple-element.847) | copy-start | bytes 12292
  216.3 12.6 %collective-permute-start.5 = (f32[544,128]{1,0:T(8,128)}, f32[544,128]{1,0:T(8,128)}, u32[]{:S(2)}, u32[]{:S(2)}) collective-permute-start(f32[544,128]{1,0:T(8,128)} %pad_maximum_fusion.15), channel_id=1, source_target_pairs={{0,4},{2,6},{4,8},{6,10},{8,12},{10,14},{1,5},{3,7},{5,9},{7,11},{... | collective-permute-start | bytes 835592 | tf_op jit(solution)/shard_map/ppermute | solution.py:12
  221.4 7.5 %collective-permute-start.6 = (f32[288,128]{1,0:T(8,128)S(1)}, f32[288,128]{1,0:T(8,128)S(1)}, u32[]{:S(2)}, u32[]{:S(2)}) collective-permute-start(f32[288,128]{1,0:T(8,128)S(1)} %pad_maximum_fusion.26), channel_id=1, source_target_pairs={{4,0},{6,2},{8,4},{10,6},{12,8},{14,10},{5,1},{7,3},{9,5},{11,7},{... | collective-permute-start | bytes 442376 | tf_op jit(solution)/shard_map/ppermute | solution.py:12
  232.3 1.9 copy-start.4
  236.7 11.4 %collective-permute-start.7 = (f32[256,128]{1,0:T(8,128)}, f32[256,128]{1,0:T(8,128)}, u32[]{:S(2)}, u32[]{:S(2)}) collective-permute-start(f32[256,128]{1,0:T(8,128)} %constant_dynamic-slice_fusion.11), channel_id=1, source_target_pairs={{8,0},{10,2},{12,4},{14,6},{9,1},{11,3},{13,5},{15,7},{24,16},{26,... | collective-permute-start | bytes 393224 | tf_op jit(solution)/shard_map/ppermute | solution.py:12
  250.5 10.7 %copy-start.27 = (f32[32,256]{1,0:T(8,128)S(1)}, f32[32,256]{1,0:T(8,128)}, u32[]{:S(2)}) copy-start(f32[32,256]{1,0:T(8,128)} %copy-done.26) | copy-start | bytes 98308
  253.7 21.0 %copy-start.44 = (f32[32,32]{1,0:T(8,128)}, f32[32,32]{1,0:T(8,128)S(1)}, u32[]{:S(2)}) copy-start(f32[32,32]{1,0:T(8,128)S(1)} %get-tuple-element.848) | copy-start | bytes 12292
  256.1 15.0 %collective-permute-start.8 = (f32[544,128]{1,0:T(8,128)}, f32[544,128]{1,0:T(8,128)}, u32[]{:S(2)}, u32[]{:S(2)}) collective-permute-start(f32[544,128]{1,0:T(8,128)} %pad_maximum_fusion.16), channel_id=1, source_target_pairs={{0,8},{2,10},{4,12},{6,14},{1,9},{3,11},{5,13},{7,15},{16,24},{18,... | collective-permute-start | bytes 835592 | tf_op jit(solution)/shard_map/ppermute | solution.py:12
  259.9 11.2 %collective-permute-start.9 = (f32[288,128]{1,0:T(8,128)S(1)}, f32[288,128]{1,0:T(8,128)}, u32[]{:S(2)}, u32[]{:S(2)}) collective-permute-start(f32[288,128]{1,0:T(8,128)S(1)} %pad_maximum_fusion.27), channel_id=1, source_target_pairs={{8,0},{10,2},{12,4},{14,6},{9,1},{11,3},{13,5},{15,7},{24,16},{26,... | collective-permute-start | bytes 442376 | tf_op jit(solution)/shard_map/ppermute | solution.py:12
  261.9 12.7 %copy-start.30 = (f32[32,256]{1,0:T(8,128)S(1)}, f32[32,256]{1,0:T(8,128)}, u32[]{:S(2)}) copy-start(f32[32,256]{1,0:T(8,128)} %get-tuple-element.1090) | copy-start | bytes 98308
  276.8 8.2 %copy-start.41 = (f32[32,32]{1,0:T(8,128)S(1)}, f32[32,32]{1,0:T(8,128)}, u32[]{:S(2)}) copy-start(f32[32,32]{1,0:T(8,128)} %convolution_subtract_fusion.16) | copy-start | bytes 12292
  537.8 163.9 %copy-start.16 = (f32[32,32]{1,0:T(8,128)}, f32[32,32]{1,0:T(8,128)S(1)}, u32[]{:S(2)}) copy-start(f32[32,32]{1,0:T(8,128)S(1)} %fusion.279) | copy-start | bytes 12292
  539.2 5.4 collective-permute-start.10
  540.5 11.7 %collective-permute-start.11 = (f32[544,128]{1,0:T(8,128)S(1)}, f32[544,128]{1,0:T(8,128)S(1)}, u32[]{:S(2)}, u32[]{:S(2)}) collective-permute-start(f32[544,128]{1,0:T(8,128)S(1)} %pad_maximum_fusion.17), channel_id=1, source_target_pairs={{8,0},{10,2},{12,4},{14,6},{9,1},{11,3},{13,5},{15,7},{24,16},{26,... | collective-permute-start | bytes 835592 | tf_op jit(solution)/shard_map/ppermute | solution.py:12
  553.1 44.9 %all-gather.7.cloned.1.call-start = ((), (), s32[]{:S(2)}) async-start(), calls=%async_computation.1 | async-start | bytes 1671168 | tf_op jit(solution)/shard_map/all_gather | solution.py:32
  560.5 0.9 copy-start.13
  562.3 10.0 %collective-permute-start.12 = (f32[544,128]{1,0:T(8,128)S(1)}, f32[544,128]{1,0:T(8,128)S(1)}, u32[]{:S(2)}, u32[]{:S(2)}) collective-permute-start(f32[544,128]{1,0:T(8,128)S(1)} %get-tuple-element.1163), channel_id=1, source_target_pairs={{0,4},{2,6},{4,8},{6,10},{8,12},{10,14},{1,5},{3,7},{5,9},{7,11},{... | collective-permute-start | bytes 835592 | tf_op jit(solution)/shard_map/ppermute | solution.py:12
  566.0 10.4 %collective-permute-start.13 = (f32[544,128]{1,0:T(8,128)S(1)}, f32[544,128]{1,0:T(8,128)S(1)}, u32[]{:S(2)}, u32[]{:S(2)}) collective-permute-start(f32[544,128]{1,0:T(8,128)S(1)} %get-tuple-element.1164), channel_id=1, source_target_pairs={{4,0},{6,2},{8,4},{10,6},{12,8},{14,10},{5,1},{7,3},{9,5},{11,7},{... | collective-permute-start | bytes 835592 | tf_op jit(solution)/shard_map/ppermute | solution.py:12
  577.4 71.3 %all-gather.9.cloned.1.call-start = ((), (), s32[]{:S(2)}) async-start(), calls=%async_computation.2 | async-start | bytes 1671168 | tf_op jit(solution)/shard_map/all_gather | solution.py:32
  601.9 35.7 %collective-permute-start.14 = (f32[544,128]{1,0:T(8,128)S(1)}, f32[544,128]{1,0:T(8,128)S(1)}, u32[]{:S(2)}, u32[]{:S(2)}) collective-permute-start(f32[544,128]{1,0:T(8,128)S(1)} %get-tuple-element.1161), channel_id=1, source_target_pairs={{0,2},{2,4},{4,6},{6,8},{8,10},{10,12},{12,14},{1,3},{3,5},{5,7},{... | collective-permute-start | bytes 835592 | tf_op jit(solution)/shard_map/ppermute | solution.py:12
  625.4 12.2 %collective-permute-start.15 = (f32[544,128]{1,0:T(8,128)S(1)}, f32[544,128]{1,0:T(8,128)S(1)}, u32[]{:S(2)}, u32[]{:S(2)}) collective-permute-start(f32[544,128]{1,0:T(8,128)S(1)} %get-tuple-element.1162), channel_id=1, source_target_pairs={{2,0},{4,2},{6,4},{8,6},{10,8},{12,10},{14,12},{3,1},{5,3},{7,5},{... | collective-permute-start | bytes 835592 | tf_op jit(solution)/shard_map/ppermute | solution.py:12
  638.4 52.6 %all-gather.11.cloned.1.call-start = ((), (), s32[]{:S(2)}) async-start(), calls=%async_computation.3 | async-start | bytes 1622016 | tf_op jit(solution)/shard_map/all_gather | solution.py:32
  658.8 2.7 copy-start.8
  667.2 3.4 copy-start.32
  669.1 7.8 %collective-permute-start.16 = (f32[544,128]{1,0:T(8,128)S(1)}, f32[544,128]{1,0:T(8,128)S(1)}, u32[]{:S(2)}, u32[]{:S(2)}) collective-permute-start(f32[544,128]{1,0:T(8,128)S(1)} %pad_maximum_fusion.22), channel_id=1, source_target_pairs={{0,2},{2,4},{4,6},{6,8},{8,10},{10,12},{12,14},{1,3},{3,5},{5,7},{... | collective-permute-start | bytes 835592 | tf_op jit(solution)/shard_map/ppermute | solution.py:12
  691.0 4.2 slice-start
  691.0 4.6 copy-start.3
  696.5 1.4 copy-start.22
  696.6 1.4 copy-start.34
  700.7 2.4 copy-start.33
  704.5 2.6 copy-start.11
  704.5 3.2 copy-start.2
  (10 other events, 6.7 us)
Sparse Core Ops, SparseCore 0:
  553.2 6.3 all-gather.4
  577.5 20.4 all-gather.6
  638.5 10.0 all-gather.8
  677.9 13.0 all-gather.10
where the time goes:
time: 735 us; the launch traced here: 724 us
  blocking collectives  264 us (36%)
  other arithmetic  149 us (20%)
  waiting for transfers between devices  122 us (17%)
  starting transfers between devices  51.5 us (7%)
  local copies, waits for them, and re-layouts  51 us (7%)
  matrix products  48.9 us (7%)
  between operations  19.3 us (3%)
  loops' own time  17.4 us (2%)
    psum x1, blocking collectives, fixed_total(): return lax.psum(local_sum, 'tm')  237 us
    ppermute x17, waiting for transfers between devices, passed_along(): return lax.ppermute(block, axis, route)  75.9 us
    another operation x16, other arithmetic, inverse_full(): factor = jnp.linalg.cholesky(matrix)  72.8 us
    ppermute x17, starting transfers between devices, passed_along(): return lax.ppermute(block, axis, route)  51.3 us
    all_gather x4, waiting for transfers between devices, assemble(): gathered = lax.all_gather(packet, 'blk', axis=1, tiled=True)  46.3 us
    another operation x12, other arithmetic, inverse_full(): return jax.scipy.linalg.cho_solve((factor, True), identity)  44.7 us
    dot_general x73, matrix products, product(): jnp.dot(multiplier, multiplicand, precision=HIGHEST, preferred_element_ty...  38.1 us
    all_gather x9, blocking collectives, assemble(): gathered = lax.all_gather(packet, 'blk', axis=1, tiled=True)  21.4 us
  transfers between devices with their start and end apart: 21, of which 17 were waited for; matrix products, arithmetic and copies ran while one was open for 2% of the time, Pallas kernels for 0%

commit v1 on v0

v1 whole, which is shorter than its diff:
```python
import functools

import jax
import jax.numpy as jnp
from jax import lax
from jax.experimental import pallas as pl
from jax.experimental.pallas import tpu as pltpu
from jax.sharding import PartitionSpec as P

HIGHEST = lax.Precision.HIGHEST
F32 = jnp.float32
BF16 = jnp.bfloat16
VMEM = pl.BlockSpec(memory_space=pltpu.VMEM)
SMEM = pl.BlockSpec(memory_space=pltpu.SMEM)
CLOSE = 1e-6
STEPS = 40


def nn(a, b):
    return lax.dot_general(
        a, b, (((1,), (0,)), ((), ())), precision=HIGHEST, preferred_element_type=F32
    )


def nt(a, b):
    return lax.dot_general(
        a, b, (((1,), (1,)), ((), ())), precision=HIGHEST, preferred_element_type=F32
    )


def coarse(a, b):
    return jnp.dot(a.astype(BF16), b.astype(BF16), preferred_element_type=F32)


def eye(n):
    return (
        lax.broadcasted_iota(jnp.int32, (n, n), 0) == lax.broadcasted_iota(jnp.int32, (n, n), 1)
    ).astype(F32)


def squares(r):
    return jnp.sum(r * r)


def safe_start(a):
    unit = eye(a.shape[0])
    diag_row = jnp.sum(a * unit, axis=0, keepdims=True)
    diag_col = jnp.sum(a * unit, axis=1, keepdims=True)
    scaled = jnp.abs(a) * lax.rsqrt(diag_row) * lax.rsqrt(diag_col)
    bound = jnp.max(jnp.sum(scaled, axis=0, keepdims=True))
    return unit / (diag_row * bound)


def series(x_ref, r_ref):
    def more(state):
        count, size = state
        return (count < 12) & (size > 1e-4)

    def step(state):
        count, _ = state
        r = r_ref[...].astype(BF16)
        x_ref[...] += jnp.dot(r, x_ref[...].astype(BF16), preferred_element_type=F32)
        r_new = jnp.dot(r, r, preferred_element_type=F32)
        r_ref[...] = r_new
        return count + 1, squares(r_new)

    lax.while_loop(more, step, (0, squares(r_ref[...])))


def polish(a, x_ref):
    unit = eye(a.shape[0])

    def more(state):
        count, size, before = state
        return (count < STEPS) & (size > CLOSE) & ((size < before) | (size > 0.5))

    def step(state):
        count, size, _ = state
        r = unit - nn(a, x_ref[...])
        new = squares(r)
        restart = (count == 0) & ~(new < 0.8)

        @pl.when(restart)
        def _():
            x_ref[...] = safe_start(a)

        @pl.when(jnp.logical_not(restart))
        def _():
            x_ref[...] += nn(x_ref[...], r)

        return count + 1, jnp.where(restart, 1e30, new), jnp.where(restart, 2e30, size)

    lax.while_loop(more, step, (0, jnp.float32(1e30), jnp.float32(2e30)))


def first_kernel(s_ref, k_ref, h_ref, z_ref, a_ref, side_ref, x_ref, r_ref):
    h = h_ref[...]
    a = s_ref[0] * k_ref[...] + s_ref[1] * h
    a_ref[...] = a
    side_ref[...] = s_ref[1] * nn(z_ref[...], h)
    start = safe_start(a)
    x_ref[...] = start
    r_ref[...] = eye(a.shape[0]) - jnp.sum(start, axis=1, keepdims=True) * a
    series(x_ref, r_ref)
    polish(a, x_ref)


def update_kernel(last, *refs):
    if last:
        a, l, u, s, xs, ss, xr, sr, a_new, s_new, delta = refs
    else:
        a, l, u, s, xs, ss, xr, sr, ls, ur, a_new, s_new, delta, l_new, u_new = refs
    lv = l[...]
    uv = u[...]
    p = nn(lv, xs[...])
    q = nn(uv, xr[...])
    d = nt(p, lv) + nt(q, uv)
    delta[...] = d
    a_new[...] = a[...] - d
    s_new[...] = s[...] - nt(ss[...], p) - nt(sr[...], q)
    if not last:
        l_new[...] = -nn(p, ls[...])
        u_new[...] = -nn(q, ur[...])


def invert_kernel(a_ref, old_ref, delta_ref, x_ref, r_ref):
    old = old_ref[...]
    x_ref[...] = old
    r_ref[...] = coarse(old, delta_ref[...])
    series(x_ref, r_ref)
    polish(a_ref[...], x_ref)


def packet_kernel(x_ref, s_ref, s0_ref, z_ref, k_ref, h_ref, y_ref, packet_ref):
    x = x_ref[...]
    y = nn(s_ref[...], x)
    y_ref[...] = y
    s0 = s0_ref[...]
    k = k_ref[...]
    h = h_ref[...]
    f = y.shape[0]
    ys = nt(y, s0)
    parts = [nt(s0, z_ref[...]) - ys, nt(nn(y, k), y), nt(nn(y, h), y), ys]
    packet_ref[pl.ds(0, f), :] = jnp.concatenate(parts, axis=1)
    row = lax.broadcasted_iota(jnp.int32, (8, 4 * f), 0)
    packet_ref[pl.ds(f, 8), :] = jnp.where(
        row == 0, jnp.sum(x * k), jnp.where(row == 1, jnp.sum(x * h), 0.0)
    )


def gauss_jordan(m):
    n = m.shape[0]
    rows = lax.broadcasted_iota(jnp.int32, (n, n), 0)
    cols = lax.broadcasted_iota(jnp.int32, (n, n), 1)
    for k in range(n):
        row = m[k : k + 1, :]
        col = m[:, k : k + 1]
        inv = 1.0 / m[k : k + 1, k : k + 1]
        row_s = row * inv
        m_next = m - col * row_s
        m_next = jnp.where(rows == k, row_s, m_next)
        m_next = jnp.where(cols == k, -col * inv, m_next)
        m = jnp.where((rows == k) & (cols == k), inv, m_next)
    return m


def finish_kernel(c_ref, all_ref, prior_ref, x_ref, y_ref, out_ref, grad_ref, fixed_ref):
    n, _, f4 = all_ref.shape
    f = f4 // 4
    extent = x_ref.shape[0]
    packets = all_ref[:, pl.ds(0, f), :]
    total = jnp.sum(packets, axis=0)[:, :f]
    m = eye(f) * prior_ref[...] + total
    sigma = gauss_jordan(m)
    fixed_ref[...] = sigma
    y = y_ref[...]
    sy = nn(sigma, y)
    out_ref[...] = x_ref[...] + lax.dot_general(
        y, sy, (((0,), (0,)), ((), ())), precision=HIGHEST, preferred_element_type=F32
    )
    tiled = jnp.concatenate([sigma] * 4, axis=1)
    v = jnp.sum(packets * tiled[None], axis=1)
    lane = lax.broadcasted_iota(jnp.int32, (n, f4), 1)

    def part(i):
        return jnp.sum(
            jnp.where((lane >= i * f) & (lane < (i + 1) * f), v, 0.0), axis=1, keepdims=True
        )

    tail = all_ref[:, pl.ds(f, 8), :]
    s_col = part(1) + tail[:, 0, 0:1]
    h_col = part(2) + tail[:, 1, 0:1]
    u_col = -part(3)
    tau, rho, noise = c_ref[0], c_ref[1], c_ref[2]
    comp = 1.0 - rho * rho
    t_col = lax.broadcasted_iota(jnp.int32, (n, 1), 0)
    a_col = jnp.where((t_col == 0) | (t_col == n - 1), 1.0, 1.0 + rho * rho)
    g_col = tau * a_col * s_col + noise * h_col + u_col - float(extent)
    j = lax.broadcasted_iota(jnp.int32, (n, n), 0)
    t = lax.broadcasted_iota(jnp.int32, (n, n), 1)
    sign = jnp.where((j + t) % 2 == 1, 1.0, -1.0)
    ahead = jnp.where(j < t, sign, 0.0)
    behind = jnp.where(j >= t, -sign, 0.0)
    weights = jnp.where(t <= n // 2, ahead, behind)
    c_row = jnp.sum(weights * g_col, axis=0, keepdims=True) / (tau * rho)
    unit = eye(n)
    s_row = jnp.sum(unit * s_col, axis=0, keepdims=True)
    h_row = jnp.sum(unit * h_col, axis=0, keepdims=True)
    u_row = jnp.sum(unit * u_col, axis=0, keepdims=True)
    t_row = lax.broadcasted_iota(jnp.int32, (1, n), 1)
    border = (t_row == 0) | (t_row == n - 1)
    a_row = jnp.where(border, 1.0, 1.0 + rho * rho)
    b_row = jnp.where(border, 0.0, 2.0 * rho * comp)
    scale = 1.0 / extent
    grad_ref[pl.ds(0, 1), :] = (tau * a_row * s_row - 2.0 * tau * rho * c_row) * scale
    grad_ref[pl.ds(1, 1), :] = (tau * b_row * s_row - 2.0 * tau * comp * c_row) * scale
    grad_ref[pl.ds(2, 1), :] = (noise * h_row + 2.0 * u_row) * scale


def shaped(*shapes):
    return [jax.ShapeDtypeStruct(s, F32) for s in shapes]


def on_device(hyper_params, space_precision, data_precision, covariates, fixed_precision):
    core = lax.axis_index("blk")
    position = lax.axis_index("tm")
    n = 2 * lax.axis_size("tm")
    half, extent = space_precision.shape
    fixed = covariates.shape[1]
    day = 2 * position + core
    axes = ("tm", "blk")
    swap = [(0, 1), (1, 0)]

    def mine(x, c):
        return lax.dynamic_index_in_dim(x, c, 0, keepdims=False)

    def joined(own, other, axis):
        low = jnp.where(core == 0, own, other)
        high = jnp.where(core == 0, other, own)
        return jnp.concatenate([low, high], axis)

    sent = jnp.concatenate([mine(data_precision, 1 - core), space_precision], 0)
    got = lax.ppermute(sent, "blk", swap)
    got_z = lax.ppermute(mine(covariates, 1 - core), "blk", swap)
    k = joined(space_precision, got[half:], 0)
    h = joined(mine(data_precision, core), got[:half], 0)
    z = joined(mine(covariates, core), got_z, 1)

    tau = jnp.exp(hyper_params[0])
    rho = jnp.tanh(hyper_params[1])
    noise = jnp.exp(hyper_params[2])
    weight = jnp.where((day == 0) | (day == n - 1), 1.0, 1.0 + rho * rho)
    scalars = jnp.stack([tau * weight, noise])
    couple = -tau * rho * k

    def gate(flag):
        return jnp.where(flag, couple, 0.0)

    square = (extent, extent)
    side = (fixed, extent)
    a, s0, x = pl.pallas_call(
        first_kernel,
        out_shape=shaped(square, side, square),
        in_specs=[SMEM, VMEM, VMEM, VMEM],
        out_specs=[VMEM] * 3,
        scratch_shapes=[pltpu.VMEM(square, F32)],
    )(scalars, k, h, z)
    s = s0
    l, u = gate(day >= 1), gate(day <= n - 2)
    ls, ur = gate(day >= 2), gate(day <= n - 3)

    distance = 1
    while distance < n:
        last = 2 * distance >= n
        up = [(i, i + distance) for i in range(n - distance)]
        down = [(i + distance, i) for i in range(n - distance)]
        if distance > 1 and not last:
            ls, ur = lax.ppermute(l, axes, up), lax.ppermute(u, axes, down)
        ss, sr = lax.ppermute(s, axes, up), lax.ppermute(s, axes, down)
        xs, xr = lax.ppermute(x, axes, up), lax.ppermute(x, axes, down)
        args = [a, l, u, s, xs, ss, xr, sr] + ([] if last else [ls, ur])
        outs = shaped(square, side, square) + ([] if last else shaped(square, square))
        res = pl.pallas_call(
            functools.partial(update_kernel, last),
            out_shape=outs,
            in_specs=[VMEM] * len(args),
            out_specs=[VMEM] * len(outs),
        )(*args)
        a, s, delta = res[:3]
        if not last:
            l, u = res[3:]
        x = pl.pallas_call(
            invert_kernel,
            out_shape=shaped(square)[0],
            in_specs=[VMEM] * 3,
            out_specs=VMEM,
            scratch_shapes=[pltpu.VMEM(square, F32)],
        )(a, x, delta)
        distance *= 2

    y, packet = pl.pallas_call(
        packet_kernel,
        out_shape=shaped(side, (fixed + 8, 4 * fixed)),
        in_specs=[VMEM] * 6,
        out_specs=[VMEM] * 2,
    )(x, s, s0, z, k, h)
    everyone = lax.all_gather(packet, axes, axis=0)
    out, grads, sigma = pl.pallas_call(
        finish_kernel,
        out_shape=shaped(square, (3, n), (fixed, fixed)),
        in_specs=[SMEM] + [VMEM] * 4,
        out_specs=[VMEM] * 3,
    )(jnp.stack([tau, rho, noise]), everyone, fixed_precision[None], x, y)
    gradients = lax.dynamic_slice_in_dim(grads, 2 * position, 2, 1)
    own_rows = lax.dynamic_slice_in_dim(out, core * half, half, 0)
    other_rows = lax.dynamic_slice_in_dim(out, (1 - core) * half, half, 0)
    got_rows = lax.ppermute(other_rows, "blk", swap)
    low = jnp.where(core == 0, own_rows, got_rows)
    high = jnp.where(core == 0, got_rows, own_rows)
    return jnp.stack([low, high]), gradients, sigma


def solution(mesh):
    in_specs = (
        P("grp"),
        P("blk", None),
        P(("grp", "tm"), "blk", None),
        P(("grp", "tm"), None, "blk"),
        P("grp"),
    )
    out_specs = (P(("grp", "tm"), "blk", None), P(None, ("grp", "tm")), P("grp", None))
    return jax.shard_map(
        on_device, mesh=mesh, in_specs=in_specs, out_specs=out_specs, check_vma=False
    )
```

time: 735 us -> 184 us (0.25); the launches traced: 724 us -> 183 us
  blocking collectives: 264 us -> 23.4 us
  other arithmetic: 149 us -> 4.43 us
  waiting for transfers between devices: 122 us -> 20.9 us
  Pallas kernels: 0 us -> 52.5 us
  matrix products: 48.9 us -> 0 us
  local copies, waits for them, and re-layouts: 51 us -> 9.73 us
  loops' own time: 17.4 us -> 0 us
  starting transfers between devices: 51.5 us -> 68.6 us
  between operations: 19.3 us -> 3.19 us
    psum x1 -> x0, blocking collectives: 237 us -> none  [fixed_total(): return lax.psum(local_sum, 'tm')]
    another operation x28 -> x4, other arithmetic: 118 us -> 1.98 us  [the longest x2 0.74 us: on_device(): return (jnp.stack([low, high]), gradients, sigma)]
    ppermute x17 -> x23, waiting for transfers between devices: 75.9 us -> 20.9 us  [the longest x8 20.9 us: on_device(): ss, sr = (lax.ppermute(s, axes, up), lax.ppermute(s, axes, down))]
    pallas_call x0 -> x11, Pallas kernels: none -> 52.5 us  [the longest x4 20.2 us: on_device(): pl.pallas_call(invert_kernel, out_shape=shaped(square)[0], in_specs=[VMEM...]
    all_gather x4 -> x0, waiting for transfers between devices: 46.3 us -> none  [assemble(): gathered = lax.all_gather(packet, 'blk', axis=1, tiled=True)]
    dot_general x75 -> x0, matrix products: 40.1 us -> none  [the longest x73 38.1 us: product(): jnp.dot(multiplier, multiplicand, precision=HIGHEST, preferred_element_ty...]
    another operation x12 -> x0, loops' own time: 17.4 us -> none  [the longest x10 16.9 us: guarded(): lax.cond(predicate, compute, lambda: jax.tree.map(jnp.zeros_like, template))]
    ppermute x17 -> x23, starting transfers between devices: 51.3 us -> 68.6 us  [the longest x8 31.6 us: on_device(): xs, xr = (lax.ppermute(x, axes, up), lax.ppermute(x, axes, down))]
  transfers between devices with their start and end apart: 21 -> 23, of which waited for: 17 -> 6; matrix products, arithmetic and copies ran while one was open for 2% -> 2% of each run, Pallas kernels for 0% -> 0%
where the time goes in v1:
time: 184 us; the launch traced here: 183 us
  starting transfers between devices  68.6 us (37%)
  Pallas kernels  52.5 us (29%)
  blocking collectives  23.4 us (13%)
  waiting for transfers between devices  20.9 us (11%)
  local copies, waits for them, and re-layouts  9.73 us (5%)
  other arithmetic  4.43 us (2%)
  between operations  3.19 us (2%)
    ppermute x8, starting transfers between devices, on_device(): xs, xr = (lax.ppermute(x, axes, up), lax.ppermute(x, axes, down))  31.6 us
    all_gather x1, blocking collectives, on_device(): everyone = lax.all_gather(packet, axes, axis=0)  23.4 us
    ppermute x8, starting transfers between devices, on_device(): ss, sr = (lax.ppermute(s, axes, up), lax.ppermute(s, axes, down))  22.8 us
    ppermute x8, waiting for transfers between devices, on_device(): ss, sr = (lax.ppermute(s, axes, up), lax.ppermute(s, axes, down))  20.9 us
    pallas_call x4, Pallas kernels, on_device(): pl.pallas_call(invert_kernel, out_shape=shaped(square)[0], in_specs=[VMEM...  20.2 us
    pallas_call x4, Pallas kernels, on_device(): pl.pallas_call(functools.partial(update_kernel, last), out_shape=outs, in...  16.7 us
    ppermute x4, starting transfers between devices, on_device(): ls, ur = (lax.ppermute(l, axes, up), lax.ppermute(u, axes, down))  13.2 us
    unnamed x67, local copies, waits for them, and re-layouts  6.45 us
  transfers between devices with their start and end apart: 23, of which 6 were waited for; matrix products, arithmetic and copies ran while one was open for 2% of the time, Pallas kernels for 0%

profile of v1, /device:TPU:0, one launch (start us, length us, event | category | flops | bytes accessed | tf_op | source)
XLA Modules:
  0.0 182.7 jit_solution(3535024451476652316)
XLA Ops:
  0.6 0.7 dynamic-slice_bitcast_fusion.1
  1.8 0.9 dynamic-slice_bitcast_fusion
  7.3 0.7 pad_maximum_fusion.2.h_ref
  8.0 1.1 multiply_select_fusion
  9.1 6.2 %shard_map.76 = (f32[256,256]{1,0:T(8,128)}, f32[32,256]{1,0:T(8,128)}, f32[256,256]{1,0:T(8,128)}) custom-call(f32[2]{0:T(128)} %pad_maximum_fusion.6.s_ref, f32[256,256]{1,0:T(8,128)} %get-tuple-element.65.k_ref, f32[256,256]{1,0:T(8,128)} %pad_maximum_fusion.2.h_ref, f32[32,256]{1,0:T(8,128)} %pad_maximum_fusion.4.z_ref), custom_call_target="tpu_custom_call" | custom-call | tf_op jit(solution)/shard_map/pallas_call | solution.py:261
  15.3 1.3 collective-permute-start.4
  16.6 3.0 %collective-permute-start.2 = (f32[256,256]{1,0:T(8,128)}, f32[256,256]{1,0:T(8,128)S(1)}, u32[]{:S(2)}, u32[]{:S(2)}) collective-permute-start(f32[256,256]{1,0:T(8,128)} %get-tuple-element.31.old_ref), channel_id=1, source_target_pairs={{0,1},{1,2},{2,3},{3,4},{4,5},{5,6},{6,7},{7,8},{8,9},{9,10},{10,1... | collective-permute-start | bytes 786440 | tf_op jit(solution)/shard_map/ppermute | solution.py:280
  19.7 1.3 collective-permute-start.5
  21.0 4.7 %collective-permute-start.3 = (f32[32,256]{1,0:T(8,128)}, f32[32,256]{1,0:T(8,128)S(1)}, u32[]{:S(2)}, u32[]{:S(2)}) collective-permute-start(f32[32,256]{1,0:T(8,128)} %get-tuple-element.30.refs_3_.s0_ref), channel_id=1, source_target_pairs={{0,1},{1,2},{2,3},{3,4},{4,5},{5,6},{6,7},{7,8},{8,9},{9,10},{10,1... | collective-permute-start | bytes 98312 | tf_op jit(solution)/shard_map/ppermute | solution.py:279
  25.7 1.0 collective-permute-done.3.refs_5_
  27.5 4.3 %shard_map.77 = (f32[256,256]{1,0:T(8,128)}, f32[32,256]{1,0:T(8,128)}, f32[256,256]{1,0:T(8,128)}, f32[256,256]{1,0:T(8,128)}, f32[256,256]{1,0:T(8,128)}) custom-call(f32[256,256]{1,0:T(8,128)} %get-tuple-element.29.refs_0_, f32[256,256]{1,0:T(8,128)} %get-tuple-element.68.refs_1_, f32[256,256]{1,0:T(8,128)} %get-tuple-element.67.refs_2_, ...), custom_call_target="tpu_custom_call" | custom-call | tf_op jit(solution)/shard_map/pallas_call | solution.py:283
  31.9 5.4 %shard_map.78.old_ref = f32[256,256]{1,0:T(8,128)} custom-call(f32[256,256]{1,0:T(8,128)} %get-tuple-element.32.a_ref.refs_0_, f32[256,256]{1,0:T(8,128)} %get-tuple-element.31.old_ref, f32[256,256]{1,0:T(8,128)} %get-tuple-element.36.delta_ref), custom_call_target="tpu_custom_call" | custom-call | tf_op jit(solution)/shard_map/pallas_call | solution.py:292
  37.3 1.3 collective-permute-start.8
  38.6 6.7 %collective-permute-start.6 = (f32[256,256]{1,0:T(8,128)}, f32[256,256]{1,0:T(8,128)S(1)}, u32[]{:S(2)}, u32[]{:S(2)}) collective-permute-start(f32[256,256]{1,0:T(8,128)} %shard_map.78.old_ref), channel_id=1, source_target_pairs={{0,2},{1,3},{2,4},{3,5},{4,6},{5,7},{6,8},{7,9},{8,10},{9,11},{10,... | collective-permute-start | bytes 786440 | tf_op jit(solution)/shard_map/ppermute | solution.py:280
  45.2 6.7 %collective-permute-start.10 = (f32[256,256]{1,0:T(8,128)S(1)}, f32[256,256]{1,0:T(8,128)S(1)}, u32[]{:S(2)}, u32[]{:S(2)}) collective-permute-start(f32[256,256]{1,0:T(8,128)S(1)} %copy-done.7), channel_id=1, source_target_pairs={{0,2},{1,3},{2,4},{3,5},{4,6},{5,7},{6,8},{7,9},{8,10},{9,11},{10,... | collective-permute-start | bytes 786440 | tf_op jit(solution)/shard_map/ppermute | solution.py:278
  51.9 1.3 collective-permute-start.11
  53.2 1.3 collective-permute-start.9
  54.5 7.3 %collective-permute-done.9.refs_7_ = f32[32,256]{1,0:T(8,128)S(1)} collective-permute-done((f32[32,256]{1,0:T(8,128)S(1)}, f32[32,256]{1,0:T(8,128)S(1)}, u32[]{:S(2)}, u32[]{:S(2)}) %collective-permute-start.9) | collective-permute-done | bytes 32800 | tf_op jit(solution)/shard_map/ppermute | solution.py:279
  61.8 4.2 %collective-permute-start.7 = (f32[32,256]{1,0:T(8,128)S(1)}, f32[32,256]{1,0:T(8,128)S(1)}, u32[]{:S(2)}, u32[]{:S(2)}) collective-permute-start(f32[32,256]{1,0:T(8,128)S(1)} %copy-done.20), channel_id=1, source_target_pairs={{0,2},{1,3},{2,4},{3,5},{4,6},{5,7},{6,8},{7,9},{8,10},{9,11},{10,... | collective-permute-start | bytes 98312 | tf_op jit(solution)/shard_map/ppermute | solution.py:279
  66.0 4.0 %collective-permute-done.7.refs_5_ = f32[32,256]{1,0:T(8,128)S(1)} collective-permute-done((f32[32,256]{1,0:T(8,128)S(1)}, f32[32,256]{1,0:T(8,128)S(1)}, u32[]{:S(2)}, u32[]{:S(2)}) %collective-permute-start.7) | collective-permute-done | bytes 32800 | tf_op jit(solution)/shard_map/ppermute | solution.py:279
  70.9 0.7 copy-done.15
  71.6 4.3 %shard_map.79 = (f32[256,256]{1,0:T(8,128)}, f32[32,256]{1,0:T(8,128)}, f32[256,256]{1,0:T(8,128)}, f32[256,256]{1,0:T(8,128)}, f32[256,256]{1,0:T(8,128)}) custom-call(f32[256,256]{1,0:T(8,128)} %get-tuple-element.32.a_ref.refs_0_, f32[256,256]{1,0:T(8,128)} %get-tuple-element.33.refs_1_, f32[256,256]{1,0:T(8,128)} %get-tuple-element.34.refs_2_, ...), custom_call_target="tpu_custom_call" | custom-call | tf_op jit(solution)/shard_map/pallas_call | solution.py:283
  76.0 5.0 %shard_map.80.old_ref = f32[256,256]{1,0:T(8,128)} custom-call(f32[256,256]{1,0:T(8,128)} %get-tuple-element.37.a_ref.refs_0_, f32[256,256]{1,0:T(8,128)} %shard_map.78.old_ref, f32[256,256]{1,0:T(8,128)} %get-tuple-element.41.delta_ref), custom_call_target="tpu_custom_call" | custom-call | tf_op jit(solution)/shard_map/pallas_call | solution.py:292
  81.0 1.3 collective-permute-start.14
  82.3 11.3 %collective-permute-start.12 = (f32[256,256]{1,0:T(8,128)}, f32[256,256]{1,0:T(8,128)S(1)}, u32[]{:S(2)}, u32[]{:S(2)}) collective-permute-start(f32[256,256]{1,0:T(8,128)} %shard_map.80.old_ref), channel_id=1, source_target_pairs={{0,4},{1,5},{2,6},{3,7},{4,8},{5,9},{6,10},{7,11},{8,12},{9,13},{1... | collective-permute-start | bytes 786440 | tf_op jit(solution)/shard_map/ppermute | solution.py:280
  93.6 3.9 %collective-permute-start.16 = (f32[256,256]{1,0:T(8,128)S(1)}, f32[256,256]{1,0:T(8,128)S(1)}, u32[]{:S(2)}, u32[]{:S(2)}) collective-permute-start(f32[256,256]{1,0:T(8,128)S(1)} %copy-done.5), channel_id=1, source_target_pairs={{0,4},{1,5},{2,6},{3,7},{4,8},{5,9},{6,10},{7,11},{8,12},{9,13},{1... | collective-permute-start | bytes 786440 | tf_op jit(solution)/shard_map/ppermute | solution.py:278
  97.6 1.3 collective-permute-start.17
  98.9 1.3 collective-permute-start.15
  100.2 6.0 %collective-permute-done.15.refs_7_ = f32[32,256]{1,0:T(8,128)S(1)} collective-permute-done((f32[32,256]{1,0:T(8,128)S(1)}, f32[32,256]{1,0:T(8,128)S(1)}, u32[]{:S(2)}, u32[]{:S(2)}) %collective-permute-start.15) | collective-permute-done | bytes 32800 | tf_op jit(solution)/shard_map/ppermute | solution.py:279
  106.2 3.3 %collective-permute-start.13 = (f32[32,256]{1,0:T(8,128)S(1)}, f32[32,256]{1,0:T(8,128)S(1)}, u32[]{:S(2)}, u32[]{:S(2)}) collective-permute-start(f32[32,256]{1,0:T(8,128)S(1)} %copy-done.19), channel_id=1, source_target_pairs={{0,4},{1,5},{2,6},{3,7},{4,8},{5,9},{6,10},{7,11},{8,12},{9,13},{1... | collective-permute-start | bytes 98312 | tf_op jit(solution)/shard_map/ppermute | solution.py:279
  109.5 1.6 collective-permute-done.13.refs_5_
  112.0 0.7 copy-done.16
  112.7 4.3 %shard_map.81 = (f32[256,256]{1,0:T(8,128)}, f32[32,256]{1,0:T(8,128)}, f32[256,256]{1,0:T(8,128)}, f32[256,256]{1,0:T(8,128)}, f32[256,256]{1,0:T(8,128)}) custom-call(f32[256,256]{1,0:T(8,128)} %get-tuple-element.37.a_ref.refs_0_, f32[256,256]{1,0:T(8,128)} %get-tuple-element.38.refs_1_, f32[256,256]{1,0:T(8,128)} %get-tuple-element.39.refs_2_, ...), custom_call_target="tpu_custom_call" | custom-call | tf_op jit(solution)/shard_map/pallas_call | solution.py:283
  117.0 5.2 %shard_map.82.old_ref = f32[256,256]{1,0:T(8,128)} custom-call(f32[256,256]{1,0:T(8,128)} %get-tuple-element.42.a_ref.refs_0_, f32[256,256]{1,0:T(8,128)} %shard_map.80.old_ref, f32[256,256]{1,0:T(8,128)} %get-tuple-element.46.delta_ref), custom_call_target="tpu_custom_call" | custom-call | tf_op jit(solution)/shard_map/pallas_call | solution.py:292
  122.2 1.3 collective-permute-start.20
  123.5 5.5 %collective-permute-start.18 = (f32[256,256]{1,0:T(8,128)}, f32[256,256]{1,0:T(8,128)S(1)}, u32[]{:S(2)}, u32[]{:S(2)}) collective-permute-start(f32[256,256]{1,0:T(8,128)} %shard_map.82.old_ref), channel_id=1, source_target_pairs={{0,8},{1,9},{2,10},{3,11},{4,12},{5,13},{6,14},{7,15},{16,24},{17,... | collective-permute-start | bytes 786440 | tf_op jit(solution)/shard_map/ppermute | solution.py:280
  128.9 1.3 collective-permute-start.21
  130.2 5.4 %collective-permute-start.19 = (f32[32,256]{1,0:T(8,128)S(1)}, f32[32,256]{1,0:T(8,128)S(1)}, u32[]{:S(2)}, u32[]{:S(2)}) collective-permute-start(f32[32,256]{1,0:T(8,128)S(1)} %copy-done.27), channel_id=1, source_target_pairs={{0,8},{1,9},{2,10},{3,11},{4,12},{5,13},{6,14},{7,15},{16,24},{17,... | collective-permute-start | bytes 98312 | tf_op jit(solution)/shard_map/ppermute | solution.py:279
  135.7 0.7 pad_maximum_fusion.5.c_ref
  136.4 0.9 collective-permute-done.19.refs_5_
  138.1 3.7 %shard_map.83 = (f32[256,256]{1,0:T(8,128)}, f32[32,256]{1,0:T(8,128)}, f32[256,256]{1,0:T(8,128)}) custom-call(f32[256,256]{1,0:T(8,128)} %get-tuple-element.42.a_ref.refs_0_, f32[256,256]{1,0:T(8,128)} %get-tuple-element.43.refs_1_, f32[256,256]{1,0:T(8,128)} %get-tuple-element.44.refs_2_, f32[32,256]{1,0:T(8,128)} %get-tuple-element.45.refs_3_, ...), custom_call_target="tpu_custom_call" | custom-call | tf_op jit(solution)/shard_map/pallas_call | solution.py:283
  141.8 4.7 %shard_map.84.x_ref = f32[256,256]{1,0:T(8,128)} custom-call(f32[256,256]{1,0:T(8,128)} %get-tuple-element.47.a_ref, f32[256,256]{1,0:T(8,128)} %shard_map.82.old_ref, f32[256,256]{1,0:T(8,128)} %get-tuple-element.48.delta_ref), custom_call_target="tpu_custom_call" | custom-call | tf_op jit(solution)/shard_map/pallas_call | solution.py:292
  146.4 3.1 %shard_map.85 = (f32[32,256]{1,0:T(8,128)}, f32[40,128]{1,0:T(8,128)}) custom-call(f32[256,256]{1,0:T(8,128)} %shard_map.84.x_ref, f32[32,256]{1,0:T(8,128)} %get-tuple-element.49.s_ref, f32[32,256]{1,0:T(8,128)} %get-tuple-element.30.refs_3_.s0_ref, f32[32,256]{1,0:T(8,128)} %pad_maximum_fusion.4.z_ref, f32[256,256]{1,0:T(8,128)} %get-tuple-element.65.k_ref, ...), custom_call_target="tpu_custom_call" | custom-call | tf_op jit(solution)/shard_map/pallas_call | solution.py:301
  149.5 23.4 %all-gather = f32[640,128]{1,0:T(8,128)} all-gather(f32[40,128]{1,0:T(8,128)} %get-tuple-element.50), channel_id=2, replica_groups=mesh['grp'=2,'tm'=8,'blk'=2] {'tm','blk'}, dimensions={0}, use_global_device_ids=true | all-gather | bytes 348160 | tf_op jit(solution)/shard_map/all_gather | solution.py:307
  172.9 6.2 %shard_map.86 = (f32[256,256]{1,0:T(8,128)}, f32[3,16]{1,0:T(4,128)}, f32[32,32]{1,0:T(8,128)}) custom-call(f32[3]{0:T(128)} %pad_maximum_fusion.5.c_ref, f32[16,40,128]{2,1,0:T(8,128)} %bitcast.19, f32[1,32]{1,0:T(1,128)} %bitcast.20, f32[256,256]{1,0:T(8,128)} %shard_map.84.x_ref, f32[32,256]{1,0:T(8,128)} %get-tuple-element.51.y_ref), custom_call_target="tpu_custom_call" | custom-call | tf_op jit(solution)/shard_map/pallas_call | solution.py:308
  179.2 1.0 constant_dynamic-slice_fusion.1
  180.6 0.7 copy-done.32
  182.0 0.7 pad_maximum_fusion.3
  (92 shorter events, 7.4 us)
Async XLA Ops:
  1.4 1.4 copy-start
  1.4 5.3 %collective-permute-start.1 = (f32[32,128]{1,0:T(8,128)S(1)}, f32[32,128]{1,0:T(8,128)S(1)}, u32[]{:S(2)}, u32[]{:S(2)}) collective-permute-start(f32[32,128]{1,0:T(8,128)S(1)} %dynamic-slice_bitcast_fusion.1), channel_id=1, source_target_pairs={{0,1},{1,0},{2,3},{3,2},{4,5},{5,4},{6,7},{7,6},{8,9},{9,8},{10,11... | collective-permute-start | bytes 49160 | tf_op jit(solution)/shard_map/ppermute | solution.py:244
  2.8 4.5 %copy-start.1 = (f32[2,128,256]{2,1,0:T(8,128)S(1)}, f32[2,128,256]{2,1,0:T(8,128)}, u32[]{:S(2)}) copy-start(f32[2,128,256]{2,1,0:T(8,128)} %param.7) | copy-start | bytes 786436
  2.8 3.9 %copy-start.30 = (f32[2,32,128]{2,1,0:T(8,128)S(1)}, f32[2,32,128]{2,1,0:T(8,128)}, u32[]{:S(2)}) copy-start(f32[2,32,128]{2,1,0:T(8,128)} %param.8) | copy-start | bytes 98308
  2.8 4.5 %collective-permute-start = (f32[256,256]{1,0:T(8,128)S(1)}, f32[256,256]{1,0:T(8,128)S(1)}, u32[]{:S(2)}, u32[]{:S(2)}) collective-permute-start(f32[256,256]{1,0:T(8,128)S(1)} %pad_maximum_fusion), channel_id=1, source_target_pairs={{0,1},{1,0},{2,3},{3,2},{4,5},{5,4},{6,7},{7,6},{8,9},{9,8},{10,11... | collective-permute-start | bytes 786440 | tf_op jit(solution)/shard_map/ppermute | solution.py:243
  15.3 11.4 %collective-permute-start.4 = (f32[256,256]{1,0:T(8,128)}, f32[256,256]{1,0:T(8,128)S(1)}, u32[]{:S(2)}, u32[]{:S(2)}) collective-permute-start(f32[256,256]{1,0:T(8,128)} %get-tuple-element.31.old_ref), channel_id=1, source_target_pairs={{1,0},{2,1},{3,2},{4,3},{5,4},{6,5},{7,6},{8,7},{9,8},{10,9},{11,1... | collective-permute-start | bytes 786440 | tf_op jit(solution)/shard_map/ppermute | solution.py:280
  16.6 10.1 %collective-permute-start.2 = (f32[256,256]{1,0:T(8,128)}, f32[256,256]{1,0:T(8,128)S(1)}, u32[]{:S(2)}, u32[]{:S(2)}) collective-permute-start(f32[256,256]{1,0:T(8,128)} %get-tuple-element.31.old_ref), channel_id=1, source_target_pairs={{0,1},{1,2},{2,3},{3,4},{4,5},{5,6},{6,7},{7,8},{8,9},{9,10},{10,1... | collective-permute-start | bytes 786440 | tf_op jit(solution)/shard_map/ppermute | solution.py:280
  19.7 6.0 %collective-permute-start.5 = (f32[32,256]{1,0:T(8,128)}, f32[32,256]{1,0:T(8,128)S(1)}, u32[]{:S(2)}, u32[]{:S(2)}) collective-permute-start(f32[32,256]{1,0:T(8,128)} %get-tuple-element.30.refs_3_.s0_ref), channel_id=1, source_target_pairs={{1,0},{2,1},{3,2},{4,3},{5,4},{6,5},{7,6},{8,7},{9,8},{10,9},{11,1... | collective-permute-start | bytes 98312 | tf_op jit(solution)/shard_map/ppermute | solution.py:279
  21.0 5.8 %collective-permute-start.3 = (f32[32,256]{1,0:T(8,128)}, f32[32,256]{1,0:T(8,128)S(1)}, u32[]{:S(2)}, u32[]{:S(2)}) collective-permute-start(f32[32,256]{1,0:T(8,128)} %get-tuple-element.30.refs_3_.s0_ref), channel_id=1, source_target_pairs={{0,1},{1,2},{2,3},{3,4},{4,5},{5,6},{6,7},{7,8},{8,9},{9,10},{10,1... | collective-permute-start | bytes 98312 | tf_op jit(solution)/shard_map/ppermute | solution.py:279
  25.7 1.1 copy-start.23
  26.7 0.7 copy-start.17
  26.7 0.8 copy-start.18
  31.9 13.3 %copy-start.7 = (f32[256,256]{1,0:T(8,128)S(1)}, f32[256,256]{1,0:T(8,128)}, u32[]{:S(2)}) copy-start(f32[256,256]{1,0:T(8,128)} %get-tuple-element.33.refs_1_) | copy-start | bytes 786436
  31.9 20.1 %copy-start.8 = (f32[256,256]{1,0:T(8,128)S(1)}, f32[256,256]{1,0:T(8,128)}, u32[]{:S(2)}) copy-start(f32[256,256]{1,0:T(8,128)} %get-tuple-element.34.refs_2_) | copy-start | bytes 786436
  31.9 21.4 %copy-start.20 = (f32[32,256]{1,0:T(8,128)S(1)}, f32[32,256]{1,0:T(8,128)}, u32[]{:S(2)}) copy-start(f32[32,256]{1,0:T(8,128)} %get-tuple-element.35.refs_3_) | copy-start | bytes 98308
  37.3 32.8 %collective-permute-start.8 = (f32[256,256]{1,0:T(8,128)}, f32[256,256]{1,0:T(8,128)S(1)}, u32[]{:S(2)}, u32[]{:S(2)}) collective-permute-start(f32[256,256]{1,0:T(8,128)} %shard_map.78.old_ref), channel_id=1, source_target_pairs={{2,0},{3,1},{4,2},{5,3},{6,4},{7,5},{8,6},{9,7},{10,8},{11,9},{12,... | collective-permute-start | bytes 786440 | tf_op jit(solution)/shard_map/ppermute | solution.py:280
  38.6 31.5 %collective-permute-start.6 = (f32[256,256]{1,0:T(8,128)}, f32[256,256]{1,0:T(8,128)S(1)}, u32[]{:S(2)}, u32[]{:S(2)}) collective-permute-start(f32[256,256]{1,0:T(8,128)} %shard_map.78.old_ref), channel_id=1, source_target_pairs={{0,2},{1,3},{2,4},{3,5},{4,6},{5,7},{6,8},{7,9},{8,10},{9,11},{10,... | collective-permute-start | bytes 786440 | tf_op jit(solution)/shard_map/ppermute | solution.py:280
  45.2 24.9 %collective-permute-start.10 = (f32[256,256]{1,0:T(8,128)S(1)}, f32[256,256]{1,0:T(8,128)S(1)}, u32[]{:S(2)}, u32[]{:S(2)}) collective-permute-start(f32[256,256]{1,0:T(8,128)S(1)} %copy-done.7), channel_id=1, source_target_pairs={{0,2},{1,3},{2,4},{3,5},{4,6},{5,7},{6,8},{7,9},{8,10},{9,11},{10,... | collective-permute-start | bytes 786440 | tf_op jit(solution)/shard_map/ppermute | solution.py:278
  51.9 18.2 %collective-permute-start.11 = (f32[256,256]{1,0:T(8,128)S(1)}, f32[256,256]{1,0:T(8,128)S(1)}, u32[]{:S(2)}, u32[]{:S(2)}) collective-permute-start(f32[256,256]{1,0:T(8,128)S(1)} %copy-done.8), channel_id=1, source_target_pairs={{2,0},{3,1},{4,2},{5,3},{6,4},{7,5},{8,6},{9,7},{10,8},{11,9},{12,... | collective-permute-start | bytes 786440 | tf_op jit(solution)/shard_map/ppermute | solution.py:278
  53.2 8.6 %collective-permute-start.9 = (f32[32,256]{1,0:T(8,128)S(1)}, f32[32,256]{1,0:T(8,128)S(1)}, u32[]{:S(2)}, u32[]{:S(2)}) collective-permute-start(f32[32,256]{1,0:T(8,128)S(1)} %copy-done.20), channel_id=1, source_target_pairs={{2,0},{3,1},{4,2},{5,3},{6,4},{7,5},{8,6},{9,7},{10,8},{11,9},{12,... | collective-permute-start | bytes 98312 | tf_op jit(solution)/shard_map/ppermute | solution.py:279
  61.8 8.3 %copy-start.21 = (f32[32,256]{1,0:T(8,128)}, f32[32,256]{1,0:T(8,128)S(1)}, u32[]{:S(2)}) copy-start(f32[32,256]{1,0:T(8,128)S(1)} %collective-permute-done.9.refs_7_) | copy-start | bytes 98308
  61.8 8.2 %collective-permute-start.7 = (f32[32,256]{1,0:T(8,128)S(1)}, f32[32,256]{1,0:T(8,128)S(1)}, u32[]{:S(2)}, u32[]{:S(2)}) collective-permute-start(f32[32,256]{1,0:T(8,128)S(1)} %copy-done.20), channel_id=1, source_target_pairs={{0,2},{1,3},{2,4},{3,5},{4,6},{5,7},{6,8},{7,9},{8,10},{9,11},{10,... | collective-permute-start | bytes 98312 | tf_op jit(solution)/shard_map/ppermute | solution.py:279
  70.1 0.7 copy-start.9
  70.1 0.8 copy-start.11
  70.1 0.9 copy-start.13
  76.0 17.6 %copy-start.5 = (f32[256,256]{1,0:T(8,128)S(1)}, f32[256,256]{1,0:T(8,128)}, u32[]{:S(2)}) copy-start(f32[256,256]{1,0:T(8,128)} %get-tuple-element.38.refs_1_) | copy-start | bytes 786436
  76.0 21.6 %copy-start.6 = (f32[256,256]{1,0:T(8,128)S(1)}, f32[256,256]{1,0:T(8,128)}, u32[]{:S(2)}) copy-start(f32[256,256]{1,0:T(8,128)} %get-tuple-element.39.refs_2_) | copy-start | bytes 786436
  76.0 22.9 %copy-start.19 = (f32[32,256]{1,0:T(8,128)S(1)}, f32[32,256]{1,0:T(8,128)}, u32[]{:S(2)}) copy-start(f32[32,256]{1,0:T(8,128)} %get-tuple-element.40.refs_3_) | copy-start | bytes 98308
  81.0 30.1 %collective-permute-start.14 = (f32[256,256]{1,0:T(8,128)}, f32[256,256]{1,0:T(8,128)S(1)}, u32[]{:S(2)}, u32[]{:S(2)}) collective-permute-start(f32[256,256]{1,0:T(8,128)} %shard_map.80.old_ref), channel_id=1, source_target_pairs={{4,0},{5,1},{6,2},{7,3},{8,4},{9,5},{10,6},{11,7},{12,8},{13,9},{1... | collective-permute-start | bytes 786440 | tf_op jit(solution)/shard_map/ppermute | solution.py:280
  82.3 28.8 %collective-permute-start.12 = (f32[256,256]{1,0:T(8,128)}, f32[256,256]{1,0:T(8,128)S(1)}, u32[]{:S(2)}, u32[]{:S(2)}) collective-permute-start(f32[256,256]{1,0:T(8,128)} %shard_map.80.old_ref), channel_id=1, source_target_pairs={{0,4},{1,5},{2,6},{3,7},{4,8},{5,9},{6,10},{7,11},{8,12},{9,13},{1... | collective-permute-start | bytes 786440 | tf_op jit(solution)/shard_map/ppermute | solution.py:280
  93.6 17.5 %collective-permute-start.16 = (f32[256,256]{1,0:T(8,128)S(1)}, f32[256,256]{1,0:T(8,128)S(1)}, u32[]{:S(2)}, u32[]{:S(2)}) collective-permute-start(f32[256,256]{1,0:T(8,128)S(1)} %copy-done.5), channel_id=1, source_target_pairs={{0,4},{1,5},{2,6},{3,7},{4,8},{5,9},{6,10},{7,11},{8,12},{9,13},{1... | collective-permute-start | bytes 786440 | tf_op jit(solution)/shard_map/ppermute | solution.py:278
  97.6 13.6 %collective-permute-start.17 = (f32[256,256]{1,0:T(8,128)S(1)}, f32[256,256]{1,0:T(8,128)S(1)}, u32[]{:S(2)}, u32[]{:S(2)}) collective-permute-start(f32[256,256]{1,0:T(8,128)S(1)} %copy-done.6), channel_id=1, source_target_pairs={{4,0},{5,1},{6,2},{7,3},{8,4},{9,5},{10,6},{11,7},{12,8},{13,9},{1... | collective-permute-start | bytes 786440 | tf_op jit(solution)/shard_map/ppermute | solution.py:278
  98.9 7.3 %collective-permute-start.15 = (f32[32,256]{1,0:T(8,128)S(1)}, f32[32,256]{1,0:T(8,128)S(1)}, u32[]{:S(2)}, u32[]{:S(2)}) collective-permute-start(f32[32,256]{1,0:T(8,128)S(1)} %copy-done.19), channel_id=1, source_target_pairs={{4,0},{5,1},{6,2},{7,3},{8,4},{9,5},{10,6},{11,7},{12,8},{13,9},{1... | collective-permute-start | bytes 98312 | tf_op jit(solution)/shard_map/ppermute | solution.py:279
  106.2 5.0 %copy-start.22 = (f32[32,256]{1,0:T(8,128)}, f32[32,256]{1,0:T(8,128)S(1)}, u32[]{:S(2)}) copy-start(f32[32,256]{1,0:T(8,128)S(1)} %collective-permute-done.15.refs_7_) | copy-start | bytes 98308
  106.2 4.9 %collective-permute-start.13 = (f32[32,256]{1,0:T(8,128)S(1)}, f32[32,256]{1,0:T(8,128)S(1)}, u32[]{:S(2)}, u32[]{:S(2)}) collective-permute-start(f32[32,256]{1,0:T(8,128)S(1)} %copy-done.19), channel_id=1, source_target_pairs={{0,4},{1,5},{2,6},{3,7},{4,8},{5,9},{6,10},{7,11},{8,12},{9,13},{1... | collective-permute-start | bytes 98312 | tf_op jit(solution)/shard_map/ppermute | solution.py:279
  111.1 0.7 copy-start.10
  111.1 0.8 copy-start.12
  111.1 0.9 copy-start.14
  117.0 11.9 %copy-start.27 = (f32[32,256]{1,0:T(8,128)S(1)}, f32[32,256]{1,0:T(8,128)}, u32[]{:S(2)}) copy-start(f32[32,256]{1,0:T(8,128)} %get-tuple-element.45.refs_3_) | copy-start | bytes 98308
  122.2 15.1 %collective-permute-start.20 = (f32[256,256]{1,0:T(8,128)}, f32[256,256]{1,0:T(8,128)S(1)}, u32[]{:S(2)}, u32[]{:S(2)}) collective-permute-start(f32[256,256]{1,0:T(8,128)} %shard_map.82.old_ref), channel_id=1, source_target_pairs={{8,0},{9,1},{10,2},{11,3},{12,4},{13,5},{14,6},{15,7},{24,16},{25,... | collective-permute-start | bytes 786440 | tf_op jit(solution)/shard_map/ppermute | solution.py:280
  123.5 13.8 %collective-permute-start.18 = (f32[256,256]{1,0:T(8,128)}, f32[256,256]{1,0:T(8,128)S(1)}, u32[]{:S(2)}, u32[]{:S(2)}) collective-permute-start(f32[256,256]{1,0:T(8,128)} %shard_map.82.old_ref), channel_id=1, source_target_pairs={{0,8},{1,9},{2,10},{3,11},{4,12},{5,13},{6,14},{7,15},{16,24},{17,... | collective-permute-start | bytes 786440 | tf_op jit(solution)/shard_map/ppermute | solution.py:280
  128.9 7.4 %collective-permute-start.21 = (f32[32,256]{1,0:T(8,128)S(1)}, f32[32,256]{1,0:T(8,128)S(1)}, u32[]{:S(2)}, u32[]{:S(2)}) collective-permute-start(f32[32,256]{1,0:T(8,128)S(1)} %copy-done.27), channel_id=1, source_target_pairs={{8,0},{9,1},{10,2},{11,3},{12,4},{13,5},{14,6},{15,7},{24,16},{25,... | collective-permute-start | bytes 98312 | tf_op jit(solution)/shard_map/ppermute | solution.py:279
  130.2 7.0 %collective-permute-start.19 = (f32[32,256]{1,0:T(8,128)S(1)}, f32[32,256]{1,0:T(8,128)S(1)}, u32[]{:S(2)}, u32[]{:S(2)}) collective-permute-start(f32[32,256]{1,0:T(8,128)S(1)} %copy-done.27), channel_id=1, source_target_pairs={{0,8},{1,9},{2,10},{3,11},{4,12},{5,13},{6,14},{7,15},{16,24},{17,... | collective-permute-start | bytes 98312 | tf_op jit(solution)/shard_map/ppermute | solution.py:279
  136.4 0.9 copy-start.28
  137.3 0.7 copy-start.3
  137.3 0.8 copy-start.4
  179.2 2.8 %copy-start.2 = (f32[256,256]{1,0:T(8,128)S(1)}, f32[256,256]{1,0:T(8,128)}, u32[]{:S(2)}) copy-start(f32[256,256]{1,0:T(8,128)} %get-tuple-element.52) | copy-start | bytes 786436
  180.2 1.8 collective-permute-start.22
  (8 other events, 5.1 us)

commit v2 on v1

v2 whole, which is shorter than its diff:
```python
import functools

import jax
import jax.numpy as jnp
from jax import lax
from jax.experimental import pallas as pl
from jax.experimental.pallas import tpu as pltpu
from jax.sharding import PartitionSpec as P

HIGHEST = lax.Precision.HIGHEST
F32 = jnp.float32
BF16 = jnp.bfloat16
VMEM = pl.BlockSpec(memory_space=pltpu.VMEM)
SMEM = pl.BlockSpec(memory_space=pltpu.SMEM)
CLOSE = 1e-6
STEPS = 40
DOUBLINGS = 5
MESH = pl.DeviceIdType.MESH


def nn(a, b):
    return lax.dot_general(
        a, b, (((1,), (0,)), ((), ())), precision=HIGHEST, preferred_element_type=F32
    )


def nt(a, b):
    return lax.dot_general(
        a, b, (((1,), (1,)), ((), ())), precision=HIGHEST, preferred_element_type=F32
    )


def eye(n):
    return (
        lax.broadcasted_iota(jnp.int32, (n, n), 0) == lax.broadcasted_iota(jnp.int32, (n, n), 1)
    ).astype(F32)


def squares(r):
    return jnp.sum(r * r)


def safe_start(a):
    unit = eye(a.shape[0])
    diag_row = jnp.sum(a * unit, axis=0, keepdims=True)
    diag_col = jnp.sum(a * unit, axis=1, keepdims=True)
    scaled = jnp.abs(a) * lax.rsqrt(diag_row) * lax.rsqrt(diag_col)
    bound = jnp.max(jnp.sum(scaled, axis=0, keepdims=True))
    return unit / (diag_row * bound)


def series(x_ref, r_ref):
    def more(state):
        count, size = state
        return (count < 12) & (size > 1e-4)

    def step(state):
        count, _ = state
        r = r_ref[...].astype(BF16)
        x_ref[...] += jnp.dot(r, x_ref[...].astype(BF16), preferred_element_type=F32)
        r_new = jnp.dot(r, r, preferred_element_type=F32)
        r_ref[...] = r_new
        return count + 1, squares(r_new)

    lax.while_loop(more, step, (0, squares(r_ref[...])))


def polish(a, x_ref):
    unit = eye(a.shape[0])

    def more(state):
        count, size, before = state
        return (count < STEPS) & (size > CLOSE) & ((size < before) | (size > 0.5))

    def step(state):
        count, size, _ = state
        r = unit - nn(a, x_ref[...])
        new = squares(r)
        restart = (count == 0) & ~(new < 0.8)

        @pl.when(restart)
        def _():
            x_ref[...] = safe_start(a)

        @pl.when(jnp.logical_not(restart))
        def _():
            x_ref[...] += nn(x_ref[...], r)

        return count + 1, jnp.where(restart, 1e30, new), jnp.where(restart, 2e30, size)

    lax.while_loop(more, step, (0, jnp.float32(1e30), jnp.float32(2e30)))


def split(a):
    high = a.astype(BF16)
    return high, (a - high.astype(F32)).astype(BF16)


def bdot(a, b):
    return jnp.dot(a, b, preferred_element_type=F32)


def three(a, b):
    ah, al = split(a)
    bh, bl = split(b)
    return bdot(ah, bh) + (bdot(ah, bl) + bdot(al, bh))


def first_kernel(a_ref, x_ref, r_ref):
    a = a_ref[...]
    start = safe_start(a)
    x_ref[...] = start
    r_ref[...] = eye(a.shape[0]) - jnp.sum(start, axis=1, keepdims=True) * a
    series(x_ref, r_ref)
    polish(a, x_ref)


def exchange_kernel(c_ref, space, data, cov, k_ref, h_ref, z_ref, a_ref, s_ref, ssem, rsem):
    core = lax.axis_index("blk")
    peer = {"blk": 1 - core}
    half = space.shape[0]
    barrier = pltpu.get_barrier_semaphore()
    pl.semaphore_signal(barrier, inc=1, device_id=peer, device_id_type=MESH)
    pl.semaphore_wait(barrier, 1)
    own = pl.ds(pl.multiple_of(core * half, half), half)
    sends = [
        (space, k_ref.at[own, :]),
        (data.at[1 - core], h_ref.at[own, :]),
        (cov.at[1 - core], z_ref.at[:, own]),
    ]
    copies = [
        pltpu.make_async_remote_copy(
            src_ref=src,
            dst_ref=dst,
            send_sem=ssem.at[i],
            recv_sem=rsem.at[i],
            device_id=peer,
            device_id_type=MESH,
        )
        for i, (src, dst) in enumerate(sends)
    ]
    for copy in copies:
        copy.start()
    k_ref[own, :] = space[...]
    h_ref[own, :] = data[core]
    z_ref[:, own] = cov[core]
    for copy in copies:
        copy.wait()
    h = h_ref[...]
    a_ref[...] = c_ref[3] * k_ref[...] + c_ref[2] * h
    s_ref[...] = c_ref[2] * nn(z_ref[...], h)


def warm_inverse(a, old, delta):
    x = old
    r = three(old, delta)
    for step in range(DOUBLINGS):
        rh, rl = split(r)
        xh, xl = split(x)
        x = x + (bdot(rh, xh) + (bdot(rh, xl) + bdot(rl, xh)))
        if step < DOUBLINGS - 1:
            r = bdot(rh, rh) + (bdot(rh, rl) + bdot(rl, rh))
    residual = eye(a.shape[0]) - nn(a, x)
    return x + three(x, residual)


def main_kernel(levels, c_ref, k_ref, h_ref, z_ref, a_in, s0_ref, x0_ref, prior_ref, *rest):
    out_ref, grad_ref, fixed_ref = rest[:3]
    xo, lo, uo, so, xs, xr, ls, ur, ss, sr, all_ref, full, ssem, rsem, psend, precv, hsem = rest[3:]
    n = 1 << levels
    core = lax.axis_index("blk")
    position = lax.axis_index("tm")
    day = 2 * position + core
    half = out_ref.shape[1]
    f = s0_ref.shape[0]

    def device(t):
        return {"tm": t // 2, "blk": t % 2}

    barrier = pltpu.get_barrier_semaphore()

    @pl.loop(1, n)
    def _(o):
        pl.semaphore_signal(
            barrier, inc=1, device_id=device((day + o) % n), device_id_type=MESH
        )

    pl.semaphore_wait(barrier, n - 1)

    def transfer(src, dst, level, slot, t):
        return pltpu.make_async_remote_copy(
            src_ref=src,
            dst_ref=dst,
            send_sem=ssem.at[level, slot],
            recv_sem=rsem.at[level, slot],
            device_id=device(t),
            device_id_type=MESH,
        )

    def route(level, which):
        d = 1 << level
        if which == 0:
            src = x0_ref if level == 0 else xo.at[level - 1]
            pair = ((src, xs.at[level]), (src, xr.at[level]))
        elif which == 1:
            src = s0_ref if level == 0 else so.at[level - 1]
            pair = ((src, ss.at[level]), (src, sr.at[level]))
        else:
            pair = ((lo.at[level], ls.at[level]), (uo.at[level], ur.at[level]))
        later = transfer(*pair[0], level, 2 * which, (day + d) % n)
        earlier = transfer(*pair[1], level, 2 * which + 1, (day + n - d) % n)
        return d, later, earlier, pair[0][1], pair[1][1]

    def send(level, which):
        d, later, earlier, low, high = route(level, which)

        @pl.when(day + d < n)
        def _():
            later.start()

        @pl.when(day >= d)
        def _():
            earlier.start()

    def receive(level, which):
        d, later, earlier, low, high = route(level, which)

        @pl.when(day >= d)
        def _():
            later.wait_recv()

        @pl.when(day < d)
        def _():
            low[...] = jnp.zeros_like(low)

        @pl.when(day + d < n)
        def _():
            earlier.wait_recv()

        @pl.when(day + d >= n)
        def _():
            high[...] = jnp.zeros_like(high)

    def sent(level, which):
        d, later, earlier, low, high = route(level, which)

        @pl.when(day + d < n)
        def _():
            later.wait_send()

        @pl.when(day >= d)
        def _():
            earlier.wait_send()

    send(0, 0)
    send(0, 1)
    k = k_ref[...]
    couple = -(c_ref[0] * c_ref[1]) * k

    def gate(flag):
        return jnp.where(flag, 1.0, 0.0) * couple

    lo[0] = gate(day >= 1)
    uo[0] = gate(day <= n - 2)
    ls[0] = gate(day >= 2)
    ur[0] = gate(day <= n - 3)
    a = a_in[...]
    s = s0_ref[...]
    x = x0_ref[...]
    for level in range(levels):
        last = level == levels - 1
        receive(level, 0)
        l = lo[level]
        u = uo[level]
        p = nn(l, xs[level])
        q = nn(u, xr[level])
        delta = nt(p, l) + nt(q, u)
        receive(level, 1)
        s = s - nt(ss[level], p) - nt(sr[level], q)
        a = a - delta
        if not last:
            so[level] = s
            send(level + 1, 1)
            if level > 0:
                receive(level, 2)
            lo[level + 1] = -nn(p, ls[level])
            uo[level + 1] = -nn(q, ur[level])
            if level + 1 < levels - 1:
                send(level + 1, 2)
        x = warm_inverse(a, x, delta)
        if not last:
            xo[level] = x
            send(level + 1, 0)

    y = nn(s, x)
    s0 = s0_ref[...]
    h = h_ref[...]
    ys = nt(y, s0)
    parts = [nt(s0, z_ref[...]) - ys, nt(nn(y, k), y), nt(nn(y, h), y), ys]
    all_ref[day, pl.ds(0, f), :] = jnp.concatenate(parts, axis=1)
    line = lax.broadcasted_iota(jnp.int32, (8, 4 * f), 0)
    all_ref[day, pl.ds(f, 8), :] = jnp.where(
        line == 0, jnp.sum(x * k), jnp.where(line == 1, jnp.sum(x * h), 0.0)
    )

    def packet(to, slot):
        return pltpu.make_async_remote_copy(
            src_ref=all_ref.at[day],
            dst_ref=all_ref.at[slot],
            send_sem=psend.at[to],
            recv_sem=precv.at[slot],
            device_id=device(to),
            device_id_type=MESH,
        )

    @pl.loop(1, n)
    def _(o):
        packet((day + o) % n, day).start()

    @pl.loop(1, n)
    def _(o):
        packet((day + o) % n, (day + o) % n).wait_recv()

    finish(c_ref, all_ref, prior_ref, x, y, full, grad_ref, fixed_ref)
    swap = pltpu.make_async_remote_copy(
        src_ref=full.at[pl.ds(pl.multiple_of((1 - core) * half, half), half), :],
        dst_ref=out_ref.at[core],
        send_sem=hsem.at[0],
        recv_sem=hsem.at[1],
        device_id={"blk": 1 - core},
        device_id_type=MESH,
    )
    swap.start()
    out_ref[core] = full[pl.ds(pl.multiple_of(core * half, half), half), :]

    @pl.loop(1, n)
    def _(o):
        packet((day + o) % n, day).wait_send()

    for level in range(levels):
        sent(level, 0)
        sent(level, 1)
        if 0 < level < levels - 1:
            sent(level, 2)
    swap.wait()


def gauss_jordan(m):
    n = m.shape[0]
    rows = lax.broadcasted_iota(jnp.int32, (n, n), 0)
    cols = lax.broadcasted_iota(jnp.int32, (n, n), 1)
    for k in range(n):
        row = m[k : k + 1, :]
        col = m[:, k : k + 1]
        inv = 1.0 / m[k : k + 1, k : k + 1]
        row_s = row * inv
        m_next = m - col * row_s
        m_next = jnp.where(rows == k, row_s, m_next)
        m_next = jnp.where(cols == k, -col * inv, m_next)
        m = jnp.where((rows == k) & (cols == k), inv, m_next)
    return m


def finish(c_ref, all_ref, prior_ref, x, y, out_ref, grad_ref, fixed_ref):
    n, _, f4 = all_ref.shape
    f = f4 // 4
    extent = x.shape[0]
    packets = all_ref[:, pl.ds(0, f), :]
    total = jnp.sum(packets, axis=0)[:, :f]
    m = eye(f) * prior_ref[...] + total
    sigma = gauss_jordan(m)
    fixed_ref[...] = sigma
    sy = nn(sigma, y)
    out_ref[...] = x + lax.dot_general(
        y, sy, (((0,), (0,)), ((), ())), precision=HIGHEST, preferred_element_type=F32
    )
    tiled = jnp.concatenate([sigma] * 4, axis=1)
    v = jnp.sum(packets * tiled[None], axis=1)
    lane = lax.broadcasted_iota(jnp.int32, (n, f4), 1)

    def part(i):
        return jnp.sum(
            jnp.where((lane >= i * f) & (lane < (i + 1) * f), v, 0.0), axis=1, keepdims=True
        )

    tail = all_ref[:, pl.ds(f, 8), :]
    s_col = part(1) + tail[:, 0, 0:1]
    h_col = part(2) + tail[:, 1, 0:1]
    u_col = -part(3)
    tau, rho, noise = c_ref[0], c_ref[1], c_ref[2]
    comp = 1.0 - rho * rho
    t_col = lax.broadcasted_iota(jnp.int32, (n, 1), 0)
    a_col = jnp.where((t_col == 0) | (t_col == n - 1), 1.0, 1.0 + rho * rho)
    g_col = tau * a_col * s_col + noise * h_col + u_col - float(extent)
    j = lax.broadcasted_iota(jnp.int32, (n, n), 0)
    t = lax.broadcasted_iota(jnp.int32, (n, n), 1)
    sign = jnp.where((j + t) % 2 == 1, 1.0, -1.0)
    ahead = jnp.where(j < t, sign, 0.0)
    behind = jnp.where(j >= t, -sign, 0.0)
    weights = jnp.where(t <= n // 2, ahead, behind)
    c_row = jnp.sum(weights * g_col, axis=0, keepdims=True) / (tau * rho)
    unit = eye(n)
    s_row = jnp.sum(unit * s_col, axis=0, keepdims=True)
    h_row = jnp.sum(unit * h_col, axis=0, keepdims=True)
    u_row = jnp.sum(unit * u_col, axis=0, keepdims=True)
    t_row = lax.broadcasted_iota(jnp.int32, (1, n), 1)
    border = (t_row == 0) | (t_row == n - 1)
    a_row = jnp.where(border, 1.0, 1.0 + rho * rho)
    b_row = jnp.where(border, 0.0, 2.0 * rho * comp)
    scale = 1.0 / extent
    rows = [
        (tau * a_row * s_row - 2.0 * tau * rho * c_row) * scale,
        (tau * b_row * s_row - 2.0 * tau * comp * c_row) * scale,
        (noise * h_row + 2.0 * u_row) * scale,
    ]
    first = 2 * lax.axis_index("tm")
    two = lax.broadcasted_iota(jnp.int32, (1, 2), 1)
    for i, row in enumerate(rows):
        low = jnp.sum(jnp.where(t_row == first, row, 0.0), axis=1, keepdims=True)
        high = jnp.sum(jnp.where(t_row == first + 1, row, 0.0), axis=1, keepdims=True)
        grad_ref[pl.ds(i, 1), :] = jnp.where(two == 0, low, high)


def shaped(*shapes):
    return [jax.ShapeDtypeStruct(s, F32) for s in shapes]


def on_device(hyper_params, space_precision, data_precision, covariates, fixed_precision):
    n = 2 * lax.axis_size("tm")
    levels = n.bit_length() - 1
    half, extent = space_precision.shape
    fixed = covariates.shape[1]
    day = 2 * lax.axis_index("tm") + lax.axis_index("blk")
    tau = jnp.exp(hyper_params[0])
    rho = jnp.tanh(hyper_params[1])
    noise = jnp.exp(hyper_params[2])
    weight = jnp.where((day == 0) | (day == n - 1), 1.0, 1.0 + rho * rho)
    scalars = jnp.stack([tau, rho, noise, tau * weight])
    square = (extent, extent)
    side = (fixed, extent)
    k, h, z, a, s0 = pl.pallas_call(
        exchange_kernel,
        out_shape=shaped(square, square, side, square, side),
        in_specs=[SMEM] + [VMEM] * 3,
        out_specs=[VMEM] * 5,
        scratch_shapes=[pltpu.SemaphoreType.DMA((3,)), pltpu.SemaphoreType.DMA((3,))],
        compiler_params=pltpu.CompilerParams(collective_id=0, has_side_effects=True),
    )(scalars, space_precision, data_precision, covariates)
    x = pl.pallas_call(
        first_kernel,
        out_shape=shaped(square)[0],
        in_specs=[VMEM],
        out_specs=VMEM,
        scratch_shapes=[pltpu.VMEM(square, F32)],
    )(a)
    return pl.pallas_call(
        functools.partial(main_kernel, levels),
        out_shape=shaped((2, half, extent), (3, 2), (fixed, fixed)),
        in_specs=[SMEM] + [VMEM] * 7,
        out_specs=[VMEM] * 3,
        scratch_shapes=[pltpu.VMEM((levels,) + square, F32)] * 3
        + [pltpu.VMEM((levels,) + side, F32)]
        + [pltpu.VMEM((levels,) + square, F32)] * 4
        + [pltpu.VMEM((levels,) + side, F32)] * 2
        + [
            pltpu.VMEM((n, fixed + 8, 4 * fixed), F32),
            pltpu.VMEM(square, F32),
            pltpu.SemaphoreType.DMA((levels, 6)),
            pltpu.SemaphoreType.DMA((levels, 6)),
            pltpu.SemaphoreType.DMA((n,)),
            pltpu.SemaphoreType.DMA((n,)),
            pltpu.SemaphoreType.DMA((2,)),
        ],
        compiler_params=pltpu.CompilerParams(
            collective_id=1, has_side_effects=True, vmem_limit_bytes=48 * 1024 * 1024
        ),
    )(scalars, k, h, z, a, s0, x, fixed_precision[None])


def solution(mesh):
    in_specs = (
        P("grp"),
        P("blk", None),
        P(("grp", "tm"), "blk", None),
        P(("grp", "tm"), None, "blk"),
        P("grp"),
    )
    out_specs = (P(("grp", "tm"), "blk", None), P(None, ("grp", "tm")), P("grp", None))
    return jax.shard_map(
        on_device, mesh=mesh, in_specs=in_specs, out_specs=out_specs, check_vma=False
    )
```

time: 184 us -> 118 us (0.64)
  starting transfers between devices: 68.6 us -> 0 us
  Pallas kernels: 52.5 us -> 107 us
  blocking collectives: 23.4 us -> 0 us
  waiting for transfers between devices: 20.9 us -> 0 us
  other arithmetic: 4.43 us -> 0.59 us
  local copies, waits for them, and re-layouts: 9.73 us -> 6.62 us
    ppermute x23 -> x0, starting transfers between devices: 68.6 us -> none  [the longest x8 31.6 us: on_device(): xs, xr = (lax.ppermute(x, axes, up), lax.ppermute(x, axes, down))]
    pallas_call x11 -> x3, Pallas kernels: 52.5 us -> 107 us  [the longest x1 97.5 us: on_device(): pl.pallas_call(functools.partial(main_kernel, levels), out_shape=shaped((...]
    all_gather x1 -> x0, blocking collectives: 23.4 us -> none  [on_device(): everyone = lax.all_gather(packet, axes, axis=0)]
    ppermute x23 -> x0, waiting for transfers between devices: 20.9 us -> none  [the longest x8 20.9 us: on_device(): ss, sr = (lax.ppermute(s, axes, up), lax.ppermute(s, axes, down))]
    unnamed x67 -> x20, local copies, waits for them, and re-layouts: 6.45 us -> 5.38 us
  transfers between devices with their start and end apart: 23 -> 0, of which waited for: 6 -> 0; matrix products, arithmetic and copies ran while one was open for 2% -> 0% of each run, Pallas kernels for 0% -> 0%
where the time goes in v2:
time: 118 us; the launch traced here: 117 us
  Pallas kernels  107 us (91%)
  local copies, waits for them, and re-layouts  6.62 us (6%)
  between operations  2.79 us (2%)
    pallas_call x1, Pallas kernels, on_device(): pl.pallas_call(functools.partial(main_kernel, levels), out_shape=shaped((...  97.5 us
    pallas_call x1, Pallas kernels, on_device(): pl.pallas_call(first_kernel, out_shape=shaped(square)[0], in_specs=[VMEM]...  6.07 us
    unnamed x20, local copies, waits for them, and re-layouts  5.38 us
    pallas_call x1, Pallas kernels, on_device(): pl.pallas_call(exchange_kernel, out_shape=shaped(square, square, side, sq...  3.62 us

profile of v2, /device:TPU:0, one launch (start us, length us, event | category | flops | bytes accessed | tf_op | source)
XLA Modules:
  0.0 117.2 jit_solution(12280366185071428862)
XLA Ops:
  0.6 0.0 copy-start.8
  0.7 0.6 copy-done.8
  1.3 0.6 fusion
  4.0 0.6 pad_maximum_fusion.c_ref
  4.5 0.0 copy-start.7
  4.5 3.6 %shard_map.76 = (f32[256,256]{1,0:T(8,128)}, f32[256,256]{1,0:T(8,128)}, f32[32,256]{1,0:T(8,128)}, f32[256,256]{1,0:T(8,128)}, f32[32,256]{1,0:T(8,128)}) custom-call(f32[4]{0:T(128)} %pad_maximum_fusion.c_ref, f32[128,256]{1,0:T(8,128)} %space.1, f32[2,128,256]{2,1,0:T(8,128)} %data.1, f32[2,32,128]{2,1,0:T(8,128)} %cov.1), custom_call_target="tpu_custom_call" | custom-call | tf_op jit(solution)/shard_map/pallas_call | solution.py:441
  8.2 0.0 copy-start.6
  8.2 0.0 copy-start
  8.2 0.0 copy-start.2
  8.2 6.1 %shard_map.77.x0_ref = f32[256,256]{1,0:T(8,128)} custom-call(f32[256,256]{1,0:T(8,128)} %get-tuple-element.11.a_ref.a_in), custom_call_target="tpu_custom_call" | custom-call | tf_op jit(solution)/shard_map/pallas_call | solution.py:449
  14.3 0.0 copy-done.7
  14.3 0.0 copy-done.6
  14.3 0.0 copy-done
  14.3 0.0 copy-done.2
  14.3 0.0 copy-start.1
  14.3 0.9 copy-done.1
  15.3 0.0 copy-start.3
  15.3 0.9 copy-done.3
  16.2 0.0 copy-start.4
  16.2 0.8 copy-done.4
  17.0 0.0 copy-start.5
  17.0 0.8 copy-done.5
  17.7 97.5 %shard_map.78 = (f32[2,128,256]{2,1,0:T(8,128)S(1)}, f32[3,2]{1,0:T(4,128)S(1)}, f32[32,32]{1,0:T(8,128)S(1)}) custom-call(f32[4]{0:T(128)S(1)} %copy-done.6, f32[256,256]{1,0:T(8,128)S(1)} %copy-done.2, f32[256,256]{1,0:T(8,128)S(1)} %copy-done.3, f32[32,256]{1,0:T(8,128)S(1)} %copy-done.4, f32[256,256]{1,0:T(8,128)S(1)} %copy-done, ...), custom_call_target="tpu_custom_call" | custom-call | tf_op jit(solution)/shard_map/pallas_call | solution.py:456
  115.2 0.6 copy.8
  115.8 0.7 copy.11
  116.5 0.6 copy.12
Async XLA Ops:
  0.6 0.7 copy-start.8
  4.5 9.7 %copy-start.7 = (f32[32]{0:T(128)S(1)}, f32[32]{0:T(128)}, u32[]{:S(2)}) copy-start(f32[32]{0:T(128)} %param.9) | copy-start | bytes 388
  8.2 6.1 %copy-start.6 = (f32[4]{0:T(128)S(1)}, f32[4]{0:T(128)}, u32[]{:S(2)}) copy-start(f32[4]{0:T(128)} %pad_maximum_fusion.c_ref) | copy-start | bytes 52
  8.2 6.1 %copy-start = (f32[256,256]{1,0:T(8,128)S(1)}, f32[256,256]{1,0:T(8,128)}, u32[]{:S(2)}) copy-start(f32[256,256]{1,0:T(8,128)} %get-tuple-element.11.a_ref.a_in) | copy-start | bytes 786436
  8.2 6.1 %copy-start.2 = (f32[256,256]{1,0:T(8,128)S(1)}, f32[256,256]{1,0:T(8,128)}, u32[]{:S(2)}) copy-start(f32[256,256]{1,0:T(8,128)} %get-tuple-element.8.k_ref) | copy-start | bytes 786436
  14.3 1.0 copy-start.1
  15.3 0.9 copy-start.3
  16.2 0.8 copy-start.4
  17.0 0.8 copy-start.5

commit v3 on v2

--- a/solution.py
+++ b/solution.py
@@ -19,15 +19,17 @@
 
 
 def nn(a, b):
-    return lax.dot_general(
-        a, b, (((1,), (0,)), ((), ())), precision=HIGHEST, preferred_element_type=F32
-    )
+    return three(a, b)
 
 
 def nt(a, b):
-    return lax.dot_general(
-        a, b, (((1,), (1,)), ((), ())), precision=HIGHEST, preferred_element_type=F32
-    )
+    ah, al = split(a)
+    bh, bl = split(b)
+    return bdot_t(ah, bh) + (bdot_t(ah, bl) + bdot_t(al, bh))
+
+
+def full_dot(a, b):
+    return jnp.dot(a, b, precision=HIGHEST, preferred_element_type=F32)
 
 
 def eye(n):
@@ -74,7 +76,7 @@
 
     def step(state):
         count, size, _ = state
-        r = unit - nn(a, x_ref[...])
+        r = unit - full_dot(a, x_ref[...])
         new = squares(r)
         restart = (count == 0) & ~(new < 0.8)
 
@@ -94,6 +96,10 @@
 def split(a):
     high = a.astype(BF16)
     return high, (a - high.astype(F32)).astype(BF16)
+
+
+def bdot_t(a, b):
+    return lax.dot_general(a, b, (((1,), (1,)), ((), ())), preferred_element_type=F32)
 
 
 def bdot(a, b):
@@ -164,9 +170,24 @@
     return x + three(x, residual)
 
 
+def pack(ref, x):
+    n = x.shape[0]
+    half = n // 2
+    ref[pl.ds(0, n), :] = x[:, :half]
+    ref[pl.ds(n, half), :] = x[half:, half:]
+
+
+def unpack(ref):
+    half = ref.shape[-1]
+    left = ref[pl.ds(0, 2 * half), :]
+    right = jnp.concatenate([left[half:, :].T, ref[pl.ds(2 * half, half), :]], axis=0)
+    return jnp.concatenate([left, right], axis=1)
+
+
 def main_kernel(levels, c_ref, k_ref, h_ref, z_ref, a_in, s0_ref, x0_ref, prior_ref, *rest):
     out_ref, grad_ref, fixed_ref = rest[:3]
-    xo, lo, uo, so, xs, xr, ls, ur, ss, sr, all_ref, full, ssem, rsem, psend, precv, hsem = rest[3:]
+    xo, lo, uo, so, xs, xr, ls, ur, ss, sr, early, all_ref, full, *sems = rest[3:]
+    ssem, rsem, psend, precv, hsem = sems
     n = 1 << levels
     core = lax.axis_index("blk")
     position = lax.axis_index("tm")
@@ -200,11 +221,13 @@
     def route(level, which):
         d = 1 << level
         if which == 0:
-            src = x0_ref if level == 0 else xo.at[level - 1]
+            src = xo.at[level]
             pair = ((src, xs.at[level]), (src, xr.at[level]))
         elif which == 1:
             src = s0_ref if level == 0 else so.at[level - 1]
             pair = ((src, ss.at[level]), (src, sr.at[level]))
+        elif level == 1:
+            pair = ((early.at[0], early.at[2]), (early.at[1], early.at[3]))
         else:
             pair = ((lo.at[level], ls.at[level]), (uo.at[level], ur.at[level]))
         later = transfer(*pair[0], level, 2 * which, (day + d) % n)
@@ -252,6 +275,7 @@
         def _():
             earlier.wait_send()
 
+    pack(xo.at[0], x0_ref[...])
     send(0, 0)
     send(0, 1)
     k = k_ref[...]
@@ -272,8 +296,8 @@
         receive(level, 0)
         l = lo[level]
         u = uo[level]
-        p = nn(l, xs[level])
-        q = nn(u, xr[level])
+        p = nn(l, unpack(xs.at[level]))
+        q = nn(u, unpack(xr.at[level]))
         delta = nt(p, l) + nt(q, u)
         receive(level, 1)
         s = s - nt(ss[level], p) - nt(sr[level], q)
@@ -283,13 +307,20 @@
             send(level + 1, 1)
             if level > 0:
                 receive(level, 2)
-            lo[level + 1] = -nn(p, ls[level])
-            uo[level + 1] = -nn(q, ur[level])
+            l_far = unpack(early.at[2]) if level == 1 else ls[level]
+            u_far = unpack(early.at[3]) if level == 1 else ur[level]
+            l_new = -nn(p, l_far)
+            u_new = -nn(q, u_far)
+            lo[level + 1] = l_new
+            uo[level + 1] = u_new
+            if level == 0:
+                pack(early.at[0], l_new)
+                pack(early.at[1], u_new)
             if level + 1 < levels - 1:
                 send(level + 1, 2)
         x = warm_inverse(a, x, delta)
         if not last:
-            xo[level] = x
+            pack(xo.at[level + 1], x)
             send(level + 1, 0)
 
     y = nn(s, x)
@@ -438,6 +469,7 @@
     scalars = jnp.stack([tau, rho, noise, tau * weight])
     square = (extent, extent)
     side = (fixed, extent)
+    packed = (extent + half, half)
     k, h, z, a, s0 = pl.pallas_call(
         exchange_kernel,
         out_shape=shaped(square, square, side, square, side),
@@ -458,10 +490,13 @@
         out_shape=shaped((2, half, extent), (3, 2), (fixed, fixed)),
         in_specs=[SMEM] + [VMEM] * 7,
         out_specs=[VMEM] * 3,
-        scratch_shapes=[pltpu.VMEM((levels,) + square, F32)] * 3
+        scratch_shapes=[pltpu.VMEM((levels,) + packed, F32)]
+        + [pltpu.VMEM((levels,) + square, F32)] * 2
         + [pltpu.VMEM((levels,) + side, F32)]
-        + [pltpu.VMEM((levels,) + square, F32)] * 4
+        + [pltpu.VMEM((levels,) + packed, F32)] * 2
+        + [pltpu.VMEM((levels,) + square, F32)] * 2
         + [pltpu.VMEM((levels,) + side, F32)] * 2
+        + [pltpu.VMEM((4,) + packed, F32)]
         + [
             pltpu.VMEM((n, fixed + 8, 4 * fixed), F32),
             pltpu.VMEM(square, F32),

time: 118 us -> 101 us (0.86)
  Pallas kernels: 107 us -> 90.2 us
    pallas_call x1, Pallas kernels: 97.5 us -> 80.7 us  [on_device(): pl.pallas_call(functools.partial(main_kernel, levels), out_shape=shaped((...]
where the time goes in v3:
time: 101 us; the launch traced here: 100 us
  Pallas kernels  90.2 us (89%)
  local copies, waits for them, and re-layouts  6.62 us (7%)
  between operations  2.79 us (3%)
    pallas_call x1, Pallas kernels, on_device(): pl.pallas_call(functools.partial(main_kernel, levels), out_shape=shaped((...  80.7 us
    pallas_call x1, Pallas kernels, on_device(): pl.pallas_call(first_kernel, out_shape=shaped(square)[0], in_specs=[VMEM]...  5.86 us
    unnamed x20, local copies, waits for them, and re-layouts  5.38 us
    pallas_call x1, Pallas kernels, on_device(): pl.pallas_call(exchange_kernel, out_shape=shaped(square, square, side, sq...  3.62 us

profile of v3, /device:TPU:0, one launch (start us, length us, event | category | flops | bytes accessed | tf_op | source)
XLA Modules:
  0.0 100.2 jit_solution(2526969370170472341)
XLA Ops:
  0.6 0.0 copy-start.8
  0.7 0.6 copy-done.8
  1.3 0.6 fusion
  4.0 0.6 pad_maximum_fusion.c_ref
  4.5 0.0 copy-start.7
  4.5 3.6 %shard_map.76 = (f32[256,256]{1,0:T(8,128)}, f32[256,256]{1,0:T(8,128)}, f32[32,256]{1,0:T(8,128)}, f32[256,256]{1,0:T(8,128)}, f32[32,256]{1,0:T(8,128)}) custom-call(f32[4]{0:T(128)} %pad_maximum_fusion.c_ref, f32[128,256]{1,0:T(8,128)} %space.1, f32[2,128,256]{2,1,0:T(8,128)} %data.1, f32[2,32,128]{2,1,0:T(8,128)} %cov.1), custom_call_target="tpu_custom_call" | custom-call | tf_op jit(solution)/shard_map/pallas_call | solution.py:473
  8.2 0.0 copy-start.6
  8.2 0.0 copy-start
  8.2 0.0 copy-start.2
  8.2 5.9 %shard_map.77.x0_ref = f32[256,256]{1,0:T(8,128)} custom-call(f32[256,256]{1,0:T(8,128)} %get-tuple-element.11.a_ref.a_in), custom_call_target="tpu_custom_call" | custom-call | tf_op jit(solution)/shard_map/pallas_call | solution.py:481
  14.1 0.0 copy-done.7
  14.1 0.0 copy-done.6
  14.1 0.0 copy-done
  14.1 0.0 copy-done.2
  14.1 0.0 copy-start.1
  14.1 0.9 copy-done.1
  15.0 0.0 copy-start.3
  15.1 0.9 copy-done.3
  16.0 0.0 copy-start.4
  16.0 0.8 copy-done.4
  16.8 0.0 copy-start.5
  16.8 0.8 copy-done.5
  17.5 80.7 %shard_map.78 = (f32[2,128,256]{2,1,0:T(8,128)S(1)}, f32[3,2]{1,0:T(4,128)S(1)}, f32[32,32]{1,0:T(8,128)S(1)}) custom-call(f32[4]{0:T(128)S(1)} %copy-done.6, f32[256,256]{1,0:T(8,128)S(1)} %copy-done.2, f32[256,256]{1,0:T(8,128)S(1)} %copy-done.3, f32[32,256]{1,0:T(8,128)S(1)} %copy-done.4, f32[256,256]{1,0:T(8,128)S(1)} %copy-done, ...), custom_call_target="tpu_custom_call" | custom-call | tf_op jit(solution)/shard_map/pallas_call | solution.py:488
  98.2 0.6 copy.8
  98.9 0.7 copy.11
  99.6 0.6 copy.12
Async XLA Ops:
  0.6 0.7 copy-start.8
  4.5 9.5 %copy-start.7 = (f32[32]{0:T(128)S(1)}, f32[32]{0:T(128)}, u32[]{:S(2)}) copy-start(f32[32]{0:T(128)} %param.9) | copy-start | bytes 388
  8.2 5.9 %copy-start.6 = (f32[4]{0:T(128)S(1)}, f32[4]{0:T(128)}, u32[]{:S(2)}) copy-start(f32[4]{0:T(128)} %pad_maximum_fusion.c_ref) | copy-start | bytes 52
  8.2 5.9 %copy-start = (f32[256,256]{1,0:T(8,128)S(1)}, f32[256,256]{1,0:T(8,128)}, u32[]{:S(2)}) copy-start(f32[256,256]{1,0:T(8,128)} %get-tuple-element.11.a_ref.a_in) | copy-start | bytes 786436
  8.2 5.9 %copy-start.2 = (f32[256,256]{1,0:T(8,128)S(1)}, f32[256,256]{1,0:T(8,128)}, u32[]{:S(2)}) copy-start(f32[256,256]{1,0:T(8,128)} %get-tuple-element.8.k_ref) | copy-start | bytes 786436
  14.1 1.0 copy-start.1
  15.0 0.9 copy-start.3
  16.0 0.8 copy-start.4
  16.8 0.8 copy-start.5

commit v4 on v3

--- a/solution.py
+++ b/solution.py
@@ -157,14 +157,14 @@
     s_ref[...] = c_ref[2] * nn(z_ref[...], h)
 
 
-def warm_inverse(a, old, delta):
+def warm_inverse(a, old, delta, doublings):
     x = old
     r = three(old, delta)
-    for step in range(DOUBLINGS):
+    for step in range(doublings):
         rh, rl = split(r)
         xh, xl = split(x)
         x = x + (bdot(rh, xh) + (bdot(rh, xl) + bdot(rl, xh)))
-        if step < DOUBLINGS - 1:
+        if step < doublings - 1:
             r = bdot(rh, rh) + (bdot(rh, rl) + bdot(rl, rh))
     residual = eye(a.shape[0]) - nn(a, x)
     return x + three(x, residual)
@@ -186,7 +186,7 @@
 
 def main_kernel(levels, c_ref, k_ref, h_ref, z_ref, a_in, s0_ref, x0_ref, prior_ref, *rest):
     out_ref, grad_ref, fixed_ref = rest[:3]
-    xo, lo, uo, so, xs, xr, ls, ur, ss, sr, early, all_ref, full, *sems = rest[3:]
+    xo, lo, uo, so, xs, xr, ls, ur, ss, sr, early, all_ref, full, gtile, *sems = rest[3:]
     ssem, rsem, psend, precv, hsem = sems
     n = 1 << levels
     core = lax.axis_index("blk")
@@ -318,7 +318,7 @@
                 pack(early.at[1], u_new)
             if level + 1 < levels - 1:
                 send(level + 1, 2)
-        x = warm_inverse(a, x, delta)
+        x = warm_inverse(a, x, delta, min(DOUBLINGS, levels - level + 2))
         if not last:
             pack(xo.at[level + 1], x)
             send(level + 1, 0)
@@ -327,11 +327,19 @@
     s0 = s0_ref[...]
     h = h_ref[...]
     ys = nt(y, s0)
-    parts = [nt(s0, z_ref[...]) - ys, nt(nn(y, k), y), nt(nn(y, h), y), ys]
-    all_ref[day, pl.ds(0, f), :] = jnp.concatenate(parts, axis=1)
-    line = lax.broadcasted_iota(jnp.int32, (8, 4 * f), 0)
-    all_ref[day, pl.ds(f, 8), :] = jnp.where(
-        line == 0, jnp.sum(x * k), jnp.where(line == 1, jnp.sum(x * h), 0.0)
+    yky = nt(nn(y, k), y)
+    yhy = nt(nn(y, h), y)
+    tau, rho, noise = c_ref[0], c_ref[1], c_ref[2]
+    border = (day == 0) | (day == n - 1)
+    space_scale = tau * jnp.where(border, 1.0, 1.0 + rho * rho)
+    s_chain = jnp.sum(jnp.sum(x * k, axis=0, keepdims=True), axis=1, keepdims=True)
+    h_chain = jnp.sum(jnp.sum(x * h, axis=0, keepdims=True), axis=1, keepdims=True)
+    both = jnp.concatenate(
+        [nt(s0, z_ref[...]) - ys, space_scale * yky + noise * yhy - ys], axis=1
+    )
+    all_ref[day, pl.ds(0, f // 2), :] = jnp.concatenate([both[: f // 2], both[f // 2 :]], axis=1)
+    all_ref[day, pl.ds(f // 2, 8), :] = jnp.broadcast_to(
+        space_scale * s_chain + noise * h_chain, (8, 4 * f)
     )
 
     def packet(to, slot):
@@ -352,7 +360,14 @@
     def _(o):
         packet((day + o) % n, (day + o) % n).wait_recv()
 
-    finish(c_ref, all_ref, prior_ref, x, y, full, grad_ref, fixed_ref)
+    heads = all_ref[:, pl.ds(0, f // 2), :]
+    total = jnp.sum(heads, axis=0)
+    total = jnp.concatenate([total[:, :f], total[:, 2 * f : 3 * f]], axis=0)
+    sigma = gauss_jordan(eye(f) * prior_ref[...] + total)
+    fixed_ref[...] = sigma
+    full[...] = x + lax.dot_general(
+        y, nn(sigma, y), (((0,), (0,)), ((), ())), precision=HIGHEST, preferred_element_type=F32
+    )
     swap = pltpu.make_async_remote_copy(
         src_ref=full.at[pl.ds(pl.multiple_of((1 - core) * half, half), half), :],
         dst_ref=out_ref.at[core],
@@ -362,6 +377,31 @@
         device_id_type=MESH,
     )
     swap.start()
+    blank = jnp.zeros((f // 2, f), F32)
+    tiled = jnp.concatenate([blank, sigma[: f // 2], blank, sigma[f // 2 :]], axis=1)
+    g_col = jnp.sum(jnp.sum(heads * tiled[None], axis=1), axis=1, keepdims=True)
+    g_col = g_col + all_ref[:, pl.ds(f // 2, 8), :][:, 0, 0:1] - float(x.shape[0])
+
+    def against(block):
+        return jnp.sum(
+            jnp.sum(block * sigma, axis=0, keepdims=True), axis=1, keepdims=True
+        )
+
+    grads = gradients_of(
+        c_ref, g_col, s_chain + against(yky), h_chain + against(yhy), -against(ys), day, x.shape[0]
+    )
+    line = lax.broadcasted_iota(jnp.int32, (8, 128), 0)
+    tile = jnp.where(line == 0, grads[0], jnp.where(line == 1, grads[1], grads[2]))
+    gtile[core] = tile
+    share = pltpu.make_async_remote_copy(
+        src_ref=gtile.at[core],
+        dst_ref=gtile.at[core],
+        send_sem=hsem.at[2],
+        recv_sem=hsem.at[3],
+        device_id={"blk": 1 - core},
+        device_id_type=MESH,
+    )
+    share.start()
     out_ref[core] = full[pl.ds(pl.multiple_of(core * half, half), half), :]
 
     @pl.loop(1, n)
@@ -373,6 +413,9 @@
         sent(level, 1)
         if 0 < level < levels - 1:
             sent(level, 2)
+    share.wait()
+    two = lax.broadcasted_iota(jnp.int32, (3, 2), 1)
+    grad_ref[...] = jnp.where(two == 0, gtile[0, pl.ds(0, 3), 0:2], gtile[1, pl.ds(0, 3), 0:2])
     swap.wait()
 
 
@@ -392,64 +435,24 @@
     return m
 
 
-def finish(c_ref, all_ref, prior_ref, x, y, out_ref, grad_ref, fixed_ref):
-    n, _, f4 = all_ref.shape
-    f = f4 // 4
-    extent = x.shape[0]
-    packets = all_ref[:, pl.ds(0, f), :]
-    total = jnp.sum(packets, axis=0)[:, :f]
-    m = eye(f) * prior_ref[...] + total
-    sigma = gauss_jordan(m)
-    fixed_ref[...] = sigma
-    sy = nn(sigma, y)
-    out_ref[...] = x + lax.dot_general(
-        y, sy, (((0,), (0,)), ((), ())), precision=HIGHEST, preferred_element_type=F32
-    )
-    tiled = jnp.concatenate([sigma] * 4, axis=1)
-    v = jnp.sum(packets * tiled[None], axis=1)
-    lane = lax.broadcasted_iota(jnp.int32, (n, f4), 1)
-
-    def part(i):
-        return jnp.sum(
-            jnp.where((lane >= i * f) & (lane < (i + 1) * f), v, 0.0), axis=1, keepdims=True
-        )
-
-    tail = all_ref[:, pl.ds(f, 8), :]
-    s_col = part(1) + tail[:, 0, 0:1]
-    h_col = part(2) + tail[:, 1, 0:1]
-    u_col = -part(3)
+def gradients_of(c_ref, g_col, s_own, h_own, u_own, day, extent):
+    n = g_col.shape[0]
     tau, rho, noise = c_ref[0], c_ref[1], c_ref[2]
     comp = 1.0 - rho * rho
-    t_col = lax.broadcasted_iota(jnp.int32, (n, 1), 0)
-    a_col = jnp.where((t_col == 0) | (t_col == n - 1), 1.0, 1.0 + rho * rho)
-    g_col = tau * a_col * s_col + noise * h_col + u_col - float(extent)
-    j = lax.broadcasted_iota(jnp.int32, (n, n), 0)
-    t = lax.broadcasted_iota(jnp.int32, (n, n), 1)
-    sign = jnp.where((j + t) % 2 == 1, 1.0, -1.0)
-    ahead = jnp.where(j < t, sign, 0.0)
-    behind = jnp.where(j >= t, -sign, 0.0)
-    weights = jnp.where(t <= n // 2, ahead, behind)
-    c_row = jnp.sum(weights * g_col, axis=0, keepdims=True) / (tau * rho)
-    unit = eye(n)
-    s_row = jnp.sum(unit * s_col, axis=0, keepdims=True)
-    h_row = jnp.sum(unit * h_col, axis=0, keepdims=True)
-    u_row = jnp.sum(unit * u_col, axis=0, keepdims=True)
-    t_row = lax.broadcasted_iota(jnp.int32, (1, n), 1)
-    border = (t_row == 0) | (t_row == n - 1)
-    a_row = jnp.where(border, 1.0, 1.0 + rho * rho)
-    b_row = jnp.where(border, 0.0, 2.0 * rho * comp)
-    scale = 1.0 / extent
-    rows = [
-        (tau * a_row * s_row - 2.0 * tau * rho * c_row) * scale,
-        (tau * b_row * s_row - 2.0 * tau * comp * c_row) * scale,
-        (noise * h_row + 2.0 * u_row) * scale,
+    j = lax.broadcasted_iota(jnp.int32, (n, 1), 0)
+    sign = jnp.where((j + day) % 2 == 1, 1.0, -1.0)
+    ahead = jnp.where(j < day, sign, 0.0)
+    behind = jnp.where(j >= day, -sign, 0.0)
+    weights = jnp.where(day <= n // 2, ahead, behind)
+    c_own = jnp.sum(weights * g_col, axis=0, keepdims=True) / (tau * rho)
+    border = (day == 0) | (day == n - 1)
+    a_day = jnp.where(border, 1.0, 1.0 + rho * rho)
+    b_day = jnp.where(border, 0.0, 2.0 * rho * comp)
+    return [
+        (tau * a_day * s_own - 2.0 * tau * rho * c_own) / extent,
+        (tau * b_day * s_own - 2.0 * tau * comp * c_own) / extent,
+        (noise * h_own + 2.0 * u_own) / extent,
     ]
-    first = 2 * lax.axis_index("tm")
-    two = lax.broadcasted_iota(jnp.int32, (1, 2), 1)
-    for i, row in enumerate(rows):
-        low = jnp.sum(jnp.where(t_row == first, row, 0.0), axis=1, keepdims=True)
-        high = jnp.sum(jnp.where(t_row == first + 1, row, 0.0), axis=1, keepdims=True)
-        grad_ref[pl.ds(i, 1), :] = jnp.where(two == 0, low, high)
 
 
 def shaped(*shapes):
@@ -498,13 +501,14 @@
         + [pltpu.VMEM((levels,) + side, F32)] * 2
         + [pltpu.VMEM((4,) + packed, F32)]
         + [
-            pltpu.VMEM((n, fixed + 8, 4 * fixed), F32),
+            pltpu.VMEM((n, fixed // 2 + 8, 4 * fixed), F32),
             pltpu.VMEM(square, F32),
+            pltpu.VMEM((2, 8, 128), F32),
             pltpu.SemaphoreType.DMA((levels, 6)),
             pltpu.SemaphoreType.DMA((levels, 6)),
             pltpu.SemaphoreType.DMA((n,)),
             pltpu.SemaphoreType.DMA((n,)),
-            pltpu.SemaphoreType.DMA((2,)),
+            pltpu.SemaphoreType.DMA((4,)),
         ],
         compiler_params=pltpu.CompilerParams(
             collective_id=1, has_side_effects=True, vmem_limit_bytes=48 * 1024 * 1024

time: 101 us -> 99.5 us (0.985)
    pallas_call x1, Pallas kernels: 80.7 us -> 79 us  [on_device(): pl.pallas_call(functools.partial(main_kernel, levels), out_shape=shaped((...]
where the time goes in v4:
time: 99.5 us; the launch traced here: 99.3 us
  Pallas kernels  89.3 us (90%)
  local copies, waits for them, and re-layouts  6.62 us (7%)
  between operations  2.79 us (3%)
    pallas_call x1, Pallas kernels, on_device(): pl.pallas_call(functools.partial(main_kernel, levels), out_shape=shaped((...  79 us
    pallas_call x1, Pallas kernels, on_device(): pl.pallas_call(first_kernel, out_shape=shaped(square)[0], in_specs=[VMEM]...  6.65 us
    unnamed x20, local copies, waits for them, and re-layouts  5.38 us
    pallas_call x1, Pallas kernels, on_device(): pl.pallas_call(exchange_kernel, out_shape=shaped(square, square, side, sq...  3.62 us

profile of v4, /device:TPU:0, one launch (start us, length us, event | category | flops | bytes accessed | tf_op | source)
XLA Modules:
  0.0 99.3 jit_solution(5427220170570905049)
XLA Ops:
  0.6 0.0 copy-start.8
  0.7 0.6 copy-done.8
  1.3 0.6 fusion
  4.0 0.6 pad_maximum_fusion.c_ref
  4.5 0.0 copy-start.7
  4.5 3.6 %shard_map.76 = (f32[256,256]{1,0:T(8,128)}, f32[256,256]{1,0:T(8,128)}, f32[32,256]{1,0:T(8,128)}, f32[256,256]{1,0:T(8,128)}, f32[32,256]{1,0:T(8,128)}) custom-call(f32[4]{0:T(128)} %pad_maximum_fusion.c_ref, f32[128,256]{1,0:T(8,128)} %space.1, f32[2,128,256]{2,1,0:T(8,128)} %data.1, f32[2,32,128]{2,1,0:T(8,128)} %cov.1), custom_call_target="tpu_custom_call" | custom-call | tf_op jit(solution)/shard_map/pallas_call | solution.py:476
  8.2 0.0 copy-start.6
  8.2 0.0 copy-start
  8.2 0.0 copy-start.2
  8.2 6.6 %shard_map.77.x0_ref = f32[256,256]{1,0:T(8,128)} custom-call(f32[256,256]{1,0:T(8,128)} %get-tuple-element.11.a_ref.a_in), custom_call_target="tpu_custom_call" | custom-call | tf_op jit(solution)/shard_map/pallas_call | solution.py:484
  14.9 0.0 copy-done.7
  14.9 0.0 copy-done.6
  14.9 0.0 copy-done
  14.9 0.0 copy-done.2
  14.9 0.0 copy-start.1
  14.9 0.9 copy-done.1
  15.8 0.0 copy-start.3
  15.8 0.9 copy-done.3
  16.8 0.0 copy-start.4
  16.8 0.8 copy-done.4
  17.5 0.0 copy-start.5
  17.5 0.8 copy-done.5
  18.3 79.0 %shard_map.78 = (f32[2,128,256]{2,1,0:T(8,128)S(1)}, f32[3,2]{1,0:T(4,128)S(1)}, f32[32,32]{1,0:T(8,128)S(1)}) custom-call(f32[4]{0:T(128)S(1)} %copy-done.6, f32[256,256]{1,0:T(8,128)S(1)} %copy-done.2, f32[256,256]{1,0:T(8,128)S(1)} %copy-done.3, f32[32,256]{1,0:T(8,128)S(1)} %copy-done.4, f32[256,256]{1,0:T(8,128)S(1)} %copy-done, ...), custom_call_target="tpu_custom_call" | custom-call | tf_op jit(solution)/shard_map/pallas_call | solution.py:491
  97.3 0.6 copy.8
  98.0 0.7 copy.11
  98.7 0.6 copy.12
Async XLA Ops:
  0.6 0.7 copy-start.8
  4.5 10.3 %copy-start.7 = (f32[32]{0:T(128)S(1)}, f32[32]{0:T(128)}, u32[]{:S(2)}) copy-start(f32[32]{0:T(128)} %param.9) | copy-start | bytes 388
  8.2 6.7 %copy-start.6 = (f32[4]{0:T(128)S(1)}, f32[4]{0:T(128)}, u32[]{:S(2)}) copy-start(f32[4]{0:T(128)} %pad_maximum_fusion.c_ref) | copy-start | bytes 52
  8.2 6.7 %copy-start = (f32[256,256]{1,0:T(8,128)S(1)}, f32[256,256]{1,0:T(8,128)}, u32[]{:S(2)}) copy-start(f32[256,256]{1,0:T(8,128)} %get-tuple-element.11.a_ref.a_in) | copy-start | bytes 786436
  8.2 6.7 %copy-start.2 = (f32[256,256]{1,0:T(8,128)S(1)}, f32[256,256]{1,0:T(8,128)}, u32[]{:S(2)}) copy-start(f32[256,256]{1,0:T(8,128)} %get-tuple-element.8.k_ref) | copy-start | bytes 786436
  14.9 1.0 copy-start.1
  15.8 0.9 copy-start.3
  16.8 0.8 copy-start.4
  17.5 0.8 copy-start.5

commit v5 on v4

--- a/solution.py
+++ b/solution.py
@@ -184,7 +184,7 @@
     return jnp.concatenate([left, right], axis=1)
 
 
-def main_kernel(levels, c_ref, k_ref, h_ref, z_ref, a_in, s0_ref, x0_ref, prior_ref, *rest):
+def main_kernel(levels, c_ref, k_ref, h_ref, z_ref, s0_ref, x0_ref, prior_ref, *rest):
     out_ref, grad_ref, fixed_ref = rest[:3]
     xo, lo, uo, so, xs, xr, ls, ur, ss, sr, early, all_ref, full, gtile, *sems = rest[3:]
     ssem, rsem, psend, precv, hsem = sems
@@ -288,12 +288,14 @@
     uo[0] = gate(day <= n - 2)
     ls[0] = gate(day >= 2)
     ur[0] = gate(day <= n - 3)
-    a = a_in[...]
+    a = c_ref[3] * k + c_ref[2] * h_ref[...]
     s = s0_ref[...]
     x = x0_ref[...]
     for level in range(levels):
         last = level == levels - 1
         receive(level, 0)
+        if 0 < level < levels - 1:
+            send(level, 2)
         l = lo[level]
         u = uo[level]
         p = nn(l, unpack(xs.at[level]))
@@ -305,6 +307,10 @@
         if not last:
             so[level] = s
             send(level + 1, 1)
+        x = warm_inverse(a, x, delta, min(DOUBLINGS, levels - level + 2))
+        if not last:
+            pack(xo.at[level + 1], x)
+            send(level + 1, 0)
             if level > 0:
                 receive(level, 2)
             l_far = unpack(early.at[2]) if level == 1 else ls[level]
@@ -316,12 +322,6 @@
             if level == 0:
                 pack(early.at[0], l_new)
                 pack(early.at[1], u_new)
-            if level + 1 < levels - 1:
-                send(level + 1, 2)
-        x = warm_inverse(a, x, delta, min(DOUBLINGS, levels - level + 2))
-        if not last:
-            pack(xo.at[level + 1], x)
-            send(level + 1, 0)
 
     y = nn(s, x)
     s0 = s0_ref[...]
@@ -491,7 +491,7 @@
     return pl.pallas_call(
         functools.partial(main_kernel, levels),
         out_shape=shaped((2, half, extent), (3, 2), (fixed, fixed)),
-        in_specs=[SMEM] + [VMEM] * 7,
+        in_specs=[SMEM] + [VMEM] * 6,
         out_specs=[VMEM] * 3,
         scratch_shapes=[pltpu.VMEM((levels,) + packed, F32)]
         + [pltpu.VMEM((levels,) + square, F32)] * 2
@@ -513,7 +513,7 @@
         compiler_params=pltpu.CompilerParams(
             collective_id=1, has_side_effects=True, vmem_limit_bytes=48 * 1024 * 1024
         ),
-    )(scalars, k, h, z, a, s0, x, fixed_precision[None])
+    )(scalars, k, h, z, s0, x, fixed_precision[None])
 
 
 def solution(mesh):

time: 99.5 us -> 93 us (0.935)
  Pallas kernels: 89.3 us -> 83.2 us
    pallas_call x1, Pallas kernels: 79 us -> 73.8 us  [on_device(): pl.pallas_call(functools.partial(main_kernel, levels), out_shape=shaped((...]
    unnamed x20 -> x18, local copies, waits for them, and re-layouts: 5.38 us -> 4.43 us
where the time goes in v5:
time: 93 us; the launch traced here: 92.3 us
  Pallas kernels  83.2 us (89%)
  local copies, waits for them, and re-layouts  5.67 us (6%)
  between operations  2.79 us (3%)
    pallas_call x1, Pallas kernels, on_device(): pl.pallas_call(functools.partial(main_kernel, levels), out_shape=shaped((...  73.8 us
    pallas_call x1, Pallas kernels, on_device(): pl.pallas_call(first_kernel, out_shape=shaped(square)[0], in_specs=[VMEM]...  5.85 us
    unnamed x18, local copies, waits for them, and re-layouts  4.43 us
    pallas_call x1, Pallas kernels, on_device(): pl.pallas_call(exchange_kernel, out_shape=shaped(square, square, side, sq...  3.63 us

profile of v5, /device:TPU:0, one launch (start us, length us, event | category | flops | bytes accessed | tf_op | source)
XLA Modules:
  0.0 92.3 jit_solution(5396930745400393342)
XLA Ops:
  0.6 0.0 copy-start.7
  0.7 0.6 copy-done.7
  1.3 0.6 fusion
  4.0 0.6 pad_maximum_fusion.c_ref
  4.5 0.0 copy-start.6
  4.5 3.6 %shard_map.76 = (f32[256,256]{1,0:T(8,128)}, f32[256,256]{1,0:T(8,128)}, f32[32,256]{1,0:T(8,128)}, f32[256,256]{1,0:T(8,128)}, f32[32,256]{1,0:T(8,128)}) custom-call(f32[4]{0:T(128)} %pad_maximum_fusion.c_ref, f32[128,256]{1,0:T(8,128)} %space.1, f32[2,128,256]{2,1,0:T(8,128)} %data.1, f32[2,32,128]{2,1,0:T(8,128)} %cov.1), custom_call_target="tpu_custom_call" | custom-call | tf_op jit(solution)/shard_map/pallas_call | solution.py:476
  8.2 0.0 copy-start.5
  8.2 0.0 copy-start.1
  8.2 0.0 copy-start.2
  8.2 5.9 %shard_map.77.x0_ref = f32[256,256]{1,0:T(8,128)} custom-call(f32[256,256]{1,0:T(8,128)} %get-tuple-element.12.a_ref), custom_call_target="tpu_custom_call" | custom-call | tf_op jit(solution)/shard_map/pallas_call | solution.py:484
  14.1 0.0 copy-done.6
  14.1 0.0 copy-done.5
  14.1 0.0 copy-done.1
  14.1 0.0 copy-done.2
  14.1 0.0 copy-start
  14.1 0.9 %copy-done = f32[256,256]{1,0:T(8,128)S(1)} copy-done((f32[256,256]{1,0:T(8,128)S(1)}, f32[256,256]{1,0:T(8,128)}, u32[]{:S(2)}) %copy-start) | copy-done | bytes 262168
  15.0 0.0 copy-start.3
  15.0 0.8 copy-done.3
  15.8 0.0 copy-start.4
  15.8 0.8 copy-done.4
  16.6 73.8 %shard_map.78 = (f32[2,128,256]{2,1,0:T(8,128)S(1)}, f32[3,2]{1,0:T(4,128)S(1)}, f32[32,32]{1,0:T(8,128)S(1)}) custom-call(f32[4]{0:T(128)S(1)} %copy-done.5, f32[256,256]{1,0:T(8,128)S(1)} %copy-done.1, f32[256,256]{1,0:T(8,128)S(1)} %copy-done.2, f32[32,256]{1,0:T(8,128)S(1)} %copy-done.3, f32[32,256]{1,0:T(8,128)S(1)} %copy-done.4, ...), custom_call_target="tpu_custom_call" | custom-call | tf_op jit(solution)/shard_map/pallas_call | solution.py:491
  90.3 0.6 copy.8
  91.0 0.7 copy.11
  91.7 0.6 copy.12
Async XLA Ops:
  0.6 0.7 copy-start.7
  4.5 9.5 %copy-start.6 = (f32[32]{0:T(128)S(1)}, f32[32]{0:T(128)}, u32[]{:S(2)}) copy-start(f32[32]{0:T(128)} %param.9) | copy-start | bytes 388
  8.2 5.9 %copy-start.5 = (f32[4]{0:T(128)S(1)}, f32[4]{0:T(128)}, u32[]{:S(2)}) copy-start(f32[4]{0:T(128)} %pad_maximum_fusion.c_ref) | copy-start | bytes 52
  8.2 5.9 %copy-start.1 = (f32[256,256]{1,0:T(8,128)S(1)}, f32[256,256]{1,0:T(8,128)}, u32[]{:S(2)}) copy-start(f32[256,256]{1,0:T(8,128)} %get-tuple-element.8.k_ref) | copy-start | bytes 786436
  8.2 5.9 %copy-start.2 = (f32[256,256]{1,0:T(8,128)S(1)}, f32[256,256]{1,0:T(8,128)}, u32[]{:S(2)}) copy-start(f32[256,256]{1,0:T(8,128)} %get-tuple-element.9.h_ref) | copy-start | bytes 786436
  14.1 1.0 %copy-start = (f32[256,256]{1,0:T(8,128)S(1)}, f32[256,256]{1,0:T(8,128)}, u32[]{:S(2)}) copy-start(f32[256,256]{1,0:T(8,128)} %shard_map.77.x0_ref) | copy-start | bytes 786436
  15.0 0.8 copy-start.3
  15.8 0.8 copy-start.4
